TPU v7x, 256 devices: a whole 4x4x8 slice. The times are simulated.
256 devices in a mesh: section: 16 (over y, x_hi, core), peer: 16 (over x_lo, z).
Axes of the slice: x: 4 (x_hi: 2, x_lo: 2; x = x_hi * 2 + x_lo), y: 4, z: 8, core: 2. Of those that a mesh axis runs over, the one named last changes fastest.
Arguments:
- inputs: bfloat16 [16, 16, 128, 5120], P('section', 'peer'), may hold values from -6 to 6
- out_grad: bfloat16 [16, 16, 128, 5120], P('section', 'peer'), may hold values from -6 to 6
- gains: float32 [16, 5120], P('section'), may hold values from 0.1 to 1.9
- down_proj: bfloat16 [16, 5120, 128], P('section'), may hold values from -0.078125 to 0.078125
- up_proj: bfloat16 [16, 128, 5120], P('section'), may hold values from -0.5 to 0.5
- wiring: int32 [16, 16, 16], replicated, may hold values from 0 to 2, as said below
- pair_mask: int32 [16], replicated, may hold values from 1 to 15
Outputs:
- next_inputs: bfloat16 [16, 16, 128, 5120], P('section', 'peer')
- returned_grad: bfloat16 [16, 16, 128, 5120], P('section', 'peer')
- grad_down: float32 [16, 16, 5120, 128], P('section', 'peer')
- grad_up: float32 [16, 16, 128, 5120], P('section', 'peer')
Inputs may be any that keep to these rules, and one draw needn't show every extreme that they name: For each section, every row and every column of wiring sums to 16; entries are 0, 1 or 2, and 2 occurs in every row and every column. `pair_mask`: 16 is a power of two; each section's mask is nonzero.
All inputs are finite; a program needn't handle non-finite values.
Results may differ from a plain program's by a relative error of at most 0.006.
Values may be sent and summed in bfloat16 or wider, within the bound.
A program may use at most 128 MiB of HBM per device.

v0:
```python
import jax
import jax.numpy as jnp
from jax import lax
from jax.sharding import PartitionSpec as P

CAP = 2


def passed_along(block, axis, distance):
    devices = range(lax.axis_size(axis))
    route = [((i - distance) % len(devices), i) for i in devices]
    return lax.ppermute(block, axis, route)


def swapped(block, axis, stride):
    count = lax.axis_size(axis)
    route = []
    for low in range(count):
        high = low | 1 << stride
        if high != low and high < count:
            route += [(low, high), (high, low)]
    return lax.ppermute(block, axis, route)


def layer(x, dy, g, down, up):
    xf = x.astype(jnp.float32)
    ms = jnp.mean(xf * xf, axis=-1, keepdims=True)
    rinv = lax.rsqrt(ms + 1e-05)
    normed = (xf * rinv * g).astype(jnp.bfloat16)
    pre = jnp.dot(normed, down, preferred_element_type=jnp.float32)
    sig = jax.nn.sigmoid(pre)
    act = (pre * sig).astype(jnp.bfloat16)
    out = (xf + jnp.dot(act, up, preferred_element_type=jnp.float32)).astype(jnp.bfloat16)
    dact = lax.dot_general(dy, up, (((1,), (1,)), ((), ())), preferred_element_type=jnp.float32)
    dpre = (dact * sig * (1.0 + pre * (1.0 - sig))).astype(jnp.bfloat16)
    gup = lax.dot_general(
        act, dy, (((0,), (0,)), ((), ())), preferred_element_type=jnp.float32
    ).astype(jnp.bfloat16)
    gdown = lax.dot_general(
        normed, dpre, (((0,), (0,)), ((), ())), preferred_element_type=jnp.float32
    ).astype(jnp.bfloat16)
    dnorm = (
        lax.dot_general(dpre, down, (((1,), (1,)), ((), ())), preferred_element_type=jnp.float32)
        * g
    )
    inner = jnp.mean(dnorm * xf, axis=-1, keepdims=True)
    dx = (dy.astype(jnp.float32) + rinv * (dnorm - xf * rinv * rinv * inner)).astype(jnp.bfloat16)
    return (out, dx, gdown, gup)


def pack_blocks(blocks, counts_vec, first_vec, slots):
    peers = counts_vec.shape[0]
    nblocks = blocks.shape[0]
    place = jnp.arange(slots, dtype=jnp.int32)
    source = first_vec[:, None] + place[None, :]
    valid = place[None, :] < counts_vec[:, None]
    select = (source[:, :, None] == jnp.arange(nblocks, dtype=jnp.int32)[None, None, :]) & valid[
        :, :, None
    ]
    select = select.astype(jnp.bfloat16).reshape(peers * slots, nblocks)
    return jnp.dot(select, blocks, preferred_element_type=jnp.float32).astype(jnp.bfloat16)


def unpack_blocks(received, counts_vec, first_vec, slots, nblocks):
    place = jnp.arange(slots, dtype=jnp.int32)
    target = (first_vec[:, None] + place[None, :]).reshape(-1)
    valid = (place[None, :] < counts_vec[:, None]).reshape(-1)
    select = (target[None, :] == jnp.arange(nblocks, dtype=jnp.int32)[:, None]) & valid[None, :]
    return jnp.dot(
        select.astype(jnp.bfloat16), received, preferred_element_type=jnp.float32
    ).astype(jnp.bfloat16)


def body(inputs, out_grad, gains, down_proj, up_proj, wiring, pair_mask):
    sections = lax.axis_size("section")
    nblocks = lax.axis_size("peer")
    section = lax.axis_index("section")
    peer = lax.axis_index("peer")
    x = inputs[0, 0]
    rows, width = x.shape
    out, dx, gdown, gup = layer(x, out_grad[0, 0], gains[0], down_proj[0], up_proj[0])
    blk_rows = rows // nblocks
    here = lax.dynamic_index_in_dim(wiring, section, 0, keepdims=False)
    before = lax.dynamic_index_in_dim(
        wiring, (section + sections - 1) % sections, 0, keepdims=False
    )
    here_start = jnp.cumsum(here, axis=1) - here
    before_col = jnp.cumsum(before, axis=0) - before
    out_blocks = out.reshape(nblocks, blk_rows * width)
    dx_blocks = dx.reshape(nblocks, blk_rows * width)
    fwd_buf = pack_blocks(out_blocks, here[peer], here_start[peer], CAP)
    back_buf = pack_blocks(dx_blocks, before[:, peer], before_col[:, peer], CAP)
    moved = passed_along(fwd_buf, "section", 1)
    got_fwd = lax.all_to_all(moved, "peer", split_axis=0, concat_axis=0, tiled=True)
    next_rows = unpack_blocks(got_fwd, before[:, peer], before_col[:, peer], CAP, nblocks)
    moved_back = passed_along(back_buf, "section", -1)
    got_back = lax.all_to_all(moved_back, "peer", split_axis=0, concat_axis=0, tiled=True)
    return_rows = unpack_blocks(got_back, here[peer], here_start[peer], CAP, nblocks)
    mask_value = pair_mask[section]
    other_down, other_up = (gdown, gup)
    for bit in range(lax.axis_size("peer").bit_length() - 1):
        swapped_down, swapped_up = swapped((other_down, other_up), "peer", bit)
        take = jnp.bitwise_and(jnp.right_shift(mask_value, bit), 1) == 1
        other_down = jnp.where(take, swapped_down, other_down)
        other_up = jnp.where(take, swapped_up, other_up)
    grad_down = (gdown.astype(jnp.float32) + other_down.astype(jnp.float32)) * 0.5
    grad_up = (gup.astype(jnp.float32) + other_up.astype(jnp.float32)) * 0.5
    return (
        next_rows.reshape(1, 1, rows, width),
        return_rows.reshape(1, 1, rows, width),
        grad_down.reshape(1, 1, grad_down.shape[0], grad_down.shape[1]),
        grad_up.reshape(1, 1, grad_up.shape[0], grad_up.shape[1]),
    )


def solution(mesh):
    placed = (
        P("section", "peer", None, None),
        P("section", "peer", None, None),
        P("section", None),
        P("section", None, None),
        P("section", None, None),
        P(),
        P(),
    )
    return jax.shard_map(
        body,
        mesh=mesh,
        in_specs=placed,
        out_specs=(
            P("section", "peer", None, None),
            P("section", "peer", None, None),
            P("section", "peer", None, None),
            P("section", "peer", None, None),
        ),
        check_vma=False,
    )
```

profile of v0, /device:TPU:14, one launch (start us, length us, event | category | flops | bytes accessed | tf_op | source)
XLA Modules:
  0.0 422.2 jit_solution(4184740477215684489)
XLA Ops:
  5.6 2.5 reshape.226
  10.1 3.8 convolution_convert_fusion.1
  21.1 2.0 fusion.13
  23.3 2.9 fusion.10
  29.0 17.8 %collective-permute-done = bf16[32,40960]{1,0:T(8,128)(2,1)} collective-permute-done((bf16[32,40960]{1,0:T(8,128)(2,1)}, bf16[32,40960]{1,0:T(8,128)(2,1)}, u32[]{:S(2)}, u32[]{:S(2)}) %collective-permute-start) | collective-permute-done | bytes 2621472 | tf_op jit(solution)/shard_map/ppermute | solution.py:12
  46.9 4.7 %all_to_all.16 = bf16[16,2,40960]{2,1,0:T(2,128)(2,1)} reshape(bf16[32,40960]{1,0:T(8,128)(2,1)} %collective-permute-done) | data formatting | bytes 5242880 | tf_op jit(solution)/shard_map/all_to_all | solution.py:94
  51.6 9.9 %all-to-all-start = ((bf16[16,2,40960]{2,1,0:T(2,128)(2,1)}), bf16[16,2,40960]{2,1,0:T(2,128)(2,1)S(1)}, u32[]{:S(2)}, u32[]{:S(2)}) async-start(bf16[16,2,40960]{2,1,0:T(2,128)(2,1)} %all_to_all.16), calls=%async_computation | async-start | bytes 5242880 | tf_op jit(solution)/shard_map/all_to_all | solution.py:94
  63.1 2.4 collective-permute-start.3
  66.6 23.0 %collective-permute-done.6 = bf16[128,5120]{1,0:T(8,128)(2,1)} collective-permute-done((bf16[128,5120]{1,0:T(8,128)(2,1)}, bf16[128,5120]{1,0:T(8,128)(2,1)}, u32[]{:S(2)}, u32[]{:S(2)}) %collective-permute-start.6) | collective-permute-done | bytes 1310752 | tf_op jit(solution)/shard_map/ppermute | solution.py:22
  91.1 5.1 %collective-permute-start.7 = (bf16[128,5120]{1,0:T(8,128)(2,1)S(1)}, bf16[128,5120]{1,0:T(8,128)(2,1)S(1)}, u32[]{:S(2)}, u32[]{:S(2)}) collective-permute-start(bf16[128,5120]{1,0:T(8,128)(2,1)S(1)} %broadcast_select_fusion), channel_id=1, source_target_pairs={{0,2},{2,0},{1,3},{3,1},{4,6},{6,4},{5,7},{7,5},{8,10},{10,8},{9,1... | collective-permute-start | bytes 3932168 | tf_op jit(solution)/shard_map/ppermute | solution.py:22
  96.8 109.4 %collective-permute-done.3 = bf16[5120,128]{1,0:T(8,128)(2,1)S(1)} collective-permute-done((bf16[5120,128]{1,0:T(8,128)(2,1)S(1)}, bf16[5120,128]{1,0:T(8,128)(2,1)S(1)}, u32[]{:S(2)}, u32[]{:S(2)}) %collective-permute-start.3) | collective-permute-done | bytes 1310752 | tf_op jit(solution)/shard_map/ppermute | solution.py:22
  207.4 3.6 collective-permute-start.4
  211.1 49.2 %collective-permute-done.7 = bf16[128,5120]{1,0:T(8,128)(2,1)S(1)} collective-permute-done((bf16[128,5120]{1,0:T(8,128)(2,1)S(1)}, bf16[128,5120]{1,0:T(8,128)(2,1)S(1)}, u32[]{:S(2)}, u32[]{:S(2)}) %collective-permute-start.7) | collective-permute-done | bytes 1310752 | tf_op jit(solution)/shard_map/ppermute | solution.py:22
  261.4 3.6 collective-permute-start.8
  265.7 4.7 %all_to_all.19 = bf16[16,2,40960]{2,1,0:T(2,128)(2,1)} reshape(bf16[32,40960]{1,0:T(8,128)(2,1)} %collective-permute-done.1) | data formatting | bytes 5242880 | tf_op jit(solution)/shard_map/all_to_all | solution.py:97
  270.5 5.5 %all-to-all-start.1 = ((bf16[16,2,40960]{2,1,0:T(2,128)(2,1)}), bf16[16,2,40960]{2,1,0:T(2,128)(2,1)}, u32[]{:S(2)}, u32[]{:S(2)}) async-start(bf16[16,2,40960]{2,1,0:T(2,128)(2,1)} %all_to_all.19), calls=%async_computation.1 | async-start | bytes 5242880 | tf_op jit(solution)/shard_map/all_to_all | solution.py:97
  277.7 74.0 %collective-permute-done.8 = bf16[128,5120]{1,0:T(8,128)(2,1)} collective-permute-done((bf16[128,5120]{1,0:T(8,128)(2,1)}, bf16[128,5120]{1,0:T(8,128)(2,1)}, u32[]{:S(2)}, u32[]{:S(2)}) %collective-permute-start.8) | collective-permute-done | bytes 1310752 | tf_op jit(solution)/shard_map/ppermute | solution.py:22
  354.5 3.5 multiply_bitcast_fusion.1
  358.0 46.5 %collective-permute-done.9 = bf16[128,5120]{1,0:T(8,128)(2,1)S(1)} collective-permute-done((bf16[128,5120]{1,0:T(8,128)(2,1)S(1)}, bf16[128,5120]{1,0:T(8,128)(2,1)S(1)}, u32[]{:S(2)}, u32[]{:S(2)}) %collective-permute-start.9) | collective-permute-done | bytes 1310752 | tf_op jit(solution)/shard_map/ppermute | solution.py:22
  404.5 3.4 multiply_bitcast_fusion
  407.8 2.5 all_to_all.18
  410.3 2.2 convolution_convert_fusion.3
  414.0 4.4 %all_to_all.21 = bf16[32,40960]{1,0:T(8,128)(2,1)} reshape(bf16[16,2,40960]{2,1,0:T(2,128)(2,1)} %all-to-all-done.1) | data formatting | bytes 5242880 | tf_op jit(solution)/shard_map/all_to_all | solution.py:97
  418.4 2.3 convolution_convert_fusion.2
  (64 shorter events, 29.5 us)
Async XLA Ops:
  0.6 1.9 copy-start
  0.6 2.1 copy-start.2
  0.7 2.1 copy-start.7
  2.7 1.3 copy-start.4
  10.1 3.9 copy-start.3
  10.1 3.9 copy-start.5
  14.0 32.9 %collective-permute-start = (bf16[32,40960]{1,0:T(8,128)(2,1)}, bf16[32,40960]{1,0:T(8,128)(2,1)}, u32[]{:S(2)}, u32[]{:S(2)}) collective-permute-start(bf16[32,40960]{1,0:T(8,128)(2,1)} %convolution_convert_fusion.1), channel_id=1, source_target_pairs={{240,0},{0,16},{16,32},{32,48},{48,64},{64,80},{80,96},{96,112},{1... | collective-permute-start | bytes 7864328 | tf_op jit(solution)/shard_map/ppermute | solution.py:12
  16.2 45.4 %collective-permute-start.2 = (bf16[5120,128]{1,0:T(8,128)(2,1)}, bf16[5120,128]{1,0:T(8,128)(2,1)}, u32[]{:S(2)}, u32[]{:S(2)}) collective-permute-start(bf16[5120,128]{1,0:T(8,128)(2,1)} %convolution_convert_fusion.5), channel_id=1, source_target_pairs={{0,1},{1,0},{2,3},{3,2},{4,5},{5,4},{6,7},{7,6},{8,9},{9,8},{10,11... | collective-permute-start | bytes 3932168 | tf_op jit(solution)/shard_map/ppermute | solution.py:22
  19.7 69.9 %collective-permute-start.6 = (bf16[128,5120]{1,0:T(8,128)(2,1)}, bf16[128,5120]{1,0:T(8,128)(2,1)}, u32[]{:S(2)}, u32[]{:S(2)}) collective-permute-start(bf16[128,5120]{1,0:T(8,128)(2,1)} %convolution_convert_fusion.4), channel_id=1, source_target_pairs={{0,1},{1,0},{2,3},{3,2},{4,5},{5,4},{6,7},{7,6},{8,9},{9,8},{10,11... | collective-permute-start | bytes 3932168 | tf_op jit(solution)/shard_map/ppermute | solution.py:22
  26.2 1.5 copy-start.8
  51.6 218.9 %all-to-all-start = ((bf16[16,2,40960]{2,1,0:T(2,128)(2,1)}), bf16[16,2,40960]{2,1,0:T(2,128)(2,1)S(1)}, u32[]{:S(2)}, u32[]{:S(2)}) async-start(bf16[16,2,40960]{2,1,0:T(2,128)(2,1)} %all_to_all.16), calls=%async_computation | async-start | bytes 5242880 | tf_op jit(solution)/shard_map/all_to_all | solution.py:94
  61.5 4.0 copy-start.6
  63.1 143.1 %collective-permute-start.3 = (bf16[5120,128]{1,0:T(8,128)(2,1)S(1)}, bf16[5120,128]{1,0:T(8,128)(2,1)S(1)}, u32[]{:S(2)}, u32[]{:S(2)}) collective-permute-start(bf16[5120,128]{1,0:T(8,128)(2,1)S(1)} %broadcast_select_fusion.3), channel_id=1, source_target_pairs={{0,2},{2,0},{1,3},{3,1},{4,6},{6,4},{5,7},{7,5},{8,10},{10,8},{9,1... | collective-permute-start | bytes 3932168 | tf_op jit(solution)/shard_map/ppermute | solution.py:22
  66.5 199.2 %collective-permute-start.1 = (bf16[32,40960]{1,0:T(8,128)(2,1)S(1)}, bf16[32,40960]{1,0:T(8,128)(2,1)}, u32[]{:S(2)}, u32[]{:S(2)}) collective-permute-start(bf16[32,40960]{1,0:T(8,128)(2,1)S(1)} %convolution_convert_fusion), channel_id=1, source_target_pairs={{16,0},{32,16},{48,32},{64,48},{80,64},{96,80},{112,96},{128,112},... | collective-permute-start | bytes 7864328 | tf_op jit(solution)/shard_map/ppermute | solution.py:12
  91.1 169.1 %collective-permute-start.7 = (bf16[128,5120]{1,0:T(8,128)(2,1)S(1)}, bf16[128,5120]{1,0:T(8,128)(2,1)S(1)}, u32[]{:S(2)}, u32[]{:S(2)}) collective-permute-start(bf16[128,5120]{1,0:T(8,128)(2,1)S(1)} %broadcast_select_fusion), channel_id=1, source_target_pairs={{0,2},{2,0},{1,3},{3,1},{4,6},{6,4},{5,7},{7,5},{8,10},{10,8},{9,1... | collective-permute-start | bytes 3932168 | tf_op jit(solution)/shard_map/ppermute | solution.py:22
  207.4 68.5 %collective-permute-start.4 = (bf16[5120,128]{1,0:T(8,128)(2,1)}, bf16[5120,128]{1,0:T(8,128)(2,1)}, u32[]{:S(2)}, u32[]{:S(2)}) collective-permute-start(bf16[5120,128]{1,0:T(8,128)(2,1)} %broadcast_select_fusion.4), channel_id=1, source_target_pairs={{0,4},{4,0},{1,5},{5,1},{2,6},{6,2},{3,7},{7,3},{8,12},{12,8},{9,1... | collective-permute-start | bytes 3932168 | tf_op jit(solution)/shard_map/ppermute | solution.py:22
  261.4 90.3 %collective-permute-start.8 = (bf16[128,5120]{1,0:T(8,128)(2,1)}, bf16[128,5120]{1,0:T(8,128)(2,1)}, u32[]{:S(2)}, u32[]{:S(2)}) collective-permute-start(bf16[128,5120]{1,0:T(8,128)(2,1)} %broadcast_select_fusion.1), channel_id=1, source_target_pairs={{0,4},{4,0},{1,5},{5,1},{2,6},{6,2},{3,7},{7,3},{8,12},{12,8},{9,1... | collective-permute-start | bytes 3932168 | tf_op jit(solution)/shard_map/ppermute | solution.py:22
  270.5 143.5 %all-to-all-start.1 = ((bf16[16,2,40960]{2,1,0:T(2,128)(2,1)}), bf16[16,2,40960]{2,1,0:T(2,128)(2,1)}, u32[]{:S(2)}, u32[]{:S(2)}) async-start(bf16[16,2,40960]{2,1,0:T(2,128)(2,1)} %all_to_all.19), calls=%async_computation.1 | async-start | bytes 5242880 | tf_op jit(solution)/shard_map/all_to_all | solution.py:97
  277.4 77.1 %collective-permute-start.5 = (bf16[5120,128]{1,0:T(8,128)(2,1)S(1)}, bf16[5120,128]{1,0:T(8,128)(2,1)S(1)}, u32[]{:S(2)}, u32[]{:S(2)}) collective-permute-start(bf16[5120,128]{1,0:T(8,128)(2,1)S(1)} %broadcast_select_fusion.5), channel_id=1, source_target_pairs={{0,8},{8,0},{1,9},{9,1},{2,10},{10,2},{3,11},{11,3},{4,12},{12,4},... | collective-permute-start | bytes 3932168 | tf_op jit(solution)/shard_map/ppermute | solution.py:22
  353.1 51.4 %collective-permute-start.9 = (bf16[128,5120]{1,0:T(8,128)(2,1)S(1)}, bf16[128,5120]{1,0:T(8,128)(2,1)S(1)}, u32[]{:S(2)}, u32[]{:S(2)}) collective-permute-start(bf16[128,5120]{1,0:T(8,128)(2,1)S(1)} %broadcast_select_fusion.2), channel_id=1, source_target_pairs={{0,8},{8,0},{1,9},{9,1},{2,10},{10,2},{3,11},{11,3},{4,12},{12,4},... | collective-permute-start | bytes 3932168 | tf_op jit(solution)/shard_map/ppermute | solution.py:22
  418.4 3.8 copy-start.1
where the time goes:
time: 423 us; the launch traced here: 422 us
  waiting for transfers between devices  320 us (76%)
  starting transfers between devices  33.3 us (8%)
  local copies, waits for them, and re-layouts  27.6 us (7%)
  other arithmetic  20.6 us (5%)
  matrix products  17.3 us (4%)
    ppermute x8, waiting for transfers between devices, swapped(): return lax.ppermute(block, axis, route)  302 us
    ppermute x2, waiting for transfers between devices, passed_along(): return lax.ppermute(block, axis, route)  17.8 us
    ppermute x8, starting transfers between devices, swapped(): return lax.ppermute(block, axis, route)  17.8 us
    all_to_all x1, starting transfers between devices, body(): lax.all_to_all(moved, 'peer', split_axis=0, concat_axis=0, tiled=True)  9.94 us
    all_to_all x2, local copies, waits for them, and re-layouts, body(): lax.all_to_all(moved_back, 'peer', split_axis=0, concat_axis=0, tiled=True)  9.17 us
  transfers between devices with their start and end apart: 12, of which 6 were waited for; matrix products, arithmetic and copies ran while one was open for 8% of the time, Pallas kernels for 0%

commit v1 on v0

v1 whole, which is shorter than its diff:
```python
import functools

import jax
import jax.numpy as jnp
from jax import lax
from jax.experimental import pallas as pl
from jax.experimental.pallas import tpu as pltpu
from jax.sharding import PartitionSpec as P

CAP = 2
MESH = pl.DeviceIdType.MESH
WIDE = 512


def layer_kernel(
    fslot, bslot, x_ref, dy_ref, g_ref, down_ref, up_ref,
    fwd_ref, back_ref, gup_ref, gdown_ref,
    normed, outs, dns, dxs, fsem, bsem,
):
    rows, width = x_ref.shape
    blocks, blk = outs.shape[0], outs.shape[1]
    rank = down_ref.shape[1]
    chunks = width // WIDE
    f32, bf16 = jnp.float32, jnp.bfloat16

    def cols(c):
        return pl.ds(pl.multiple_of(c * WIDE, WIDE), WIDE)

    def squares(c, total):
        xc = x_ref[:, cols(c)].astype(f32)
        return total + jnp.sum(xc * xc, axis=1, keepdims=True)

    ms = lax.fori_loop(0, chunks, squares, jnp.zeros((rows, 1), f32)) / width
    rinv = lax.rsqrt(ms + 1e-05)

    def project(c, carry):
        pre, dact = carry
        at = cols(c)
        nc = (x_ref[:, at].astype(f32) * rinv * g_ref[:, at]).astype(bf16)
        normed[:, at] = nc
        pre = pre + jnp.dot(nc, down_ref[at, :], preferred_element_type=f32)
        dact = dact + lax.dot_general(
            dy_ref[:, at], up_ref[:, at], (((1,), (1,)), ((), ())), preferred_element_type=f32
        )
        return pre, dact

    zero = jnp.zeros((rows, rank), f32)
    pre, dact = lax.fori_loop(0, chunks, project, (zero, zero))
    sig = jax.nn.sigmoid(pre)
    act = (pre * sig).astype(bf16)
    dpre = (dact * sig * (1.0 + pre * (1.0 - sig))).astype(bf16)

    def grads(c, inner):
        at = cols(c)
        xc = x_ref[:, at].astype(f32)
        gup_ref[:, at] = lax.dot_general(
            act, dy_ref[:, at], (((0,), (0,)), ((), ())), preferred_element_type=f32
        ).astype(bf16)
        gdown_ref[at, :] = lax.dot_general(
            normed[:, at], dpre, (((0,), (0,)), ((), ())), preferred_element_type=f32
        ).astype(bf16)
        oc = xc + jnp.dot(act, up_ref[:, at], preferred_element_type=f32)
        outs[:, :, at] = oc.reshape(blocks, blk, WIDE).astype(bf16)
        dn = (
            lax.dot_general(
                dpre, down_ref[at, :], (((1,), (1,)), ((), ())), preferred_element_type=f32
            )
            * g_ref[:, at]
        )
        dns[:, at] = dn
        return inner + jnp.sum(dn * xc, axis=1, keepdims=True)

    inner = lax.fori_loop(0, chunks, grads, jnp.zeros((rows, 1), f32)) / width

    def fwd_copy(i):
        return pltpu.make_async_copy(outs.at[fslot[i]], fwd_ref.at[i], fsem.at[i])

    def back_copy(i):
        return pltpu.make_async_copy(dxs.at[bslot[i]], back_ref.at[i], bsem.at[i])

    slots = fwd_ref.shape[0]
    pl.loop(0, slots)(lambda i: fwd_copy(i).start())
    pull = rinv * rinv * inner

    @pl.loop(0, chunks)
    def _(c):
        at = cols(c)
        xc = x_ref[:, at].astype(f32)
        dxc = dy_ref[:, at].astype(f32) + rinv * (dns[:, at] - xc * pull)
        dxs[:, :, at] = dxc.reshape(blocks, blk, WIDE).astype(bf16)

    pl.loop(0, slots)(lambda i: back_copy(i).start())
    pl.loop(0, slots)(lambda i: fwd_copy(i).wait())
    pl.loop(0, slots)(lambda i: back_copy(i).wait())


def layer(x, dy, g, down, up, fslot, bslot, blocks):
    rows, width = x.shape
    rank = down.shape[1]
    blk = rows // blocks
    vmem = pl.BlockSpec(memory_space=pltpu.VMEM)
    smem = pl.BlockSpec(memory_space=pltpu.SMEM)
    hbm = pl.BlockSpec(memory_space=pl.ANY)
    slots = blocks * CAP
    bf16 = jnp.bfloat16
    return pl.pallas_call(
        layer_kernel,
        name="adapter",
        in_specs=[smem, smem, vmem, vmem, vmem, vmem, vmem],
        out_specs=[hbm, hbm, vmem, vmem],
        out_shape=[
            jax.ShapeDtypeStruct((slots, blk, width), bf16),
            jax.ShapeDtypeStruct((slots, blk, width), bf16),
            jax.ShapeDtypeStruct((rank, width), bf16),
            jax.ShapeDtypeStruct((width, rank), bf16),
        ],
        scratch_shapes=[
            pltpu.VMEM((rows, width), bf16),
            pltpu.VMEM((blocks, blk, width), bf16),
            pltpu.VMEM((rows, width), jnp.float32),
            pltpu.VMEM((blocks, blk, width), bf16),
            pltpu.SemaphoreType.DMA((slots,)),
            pltpu.SemaphoreType.DMA((slots,)),
        ],
    )(fslot, bslot, x, dy, g, down, up)


def exchange_kernel(
    sections, peers, mask_ref, fwd, back, up, down,
    fwd_out, back_out, up_out, down_out,
    up_got, down_got, up_send, down_send,
    sems_f, sems_b, sems_u, sems_d, sems_u2, sems_d2, own_sem,
):
    section = lax.axis_index("section")
    me = lax.axis_index("peer")
    after = lax.rem(section + 1, sections)
    ahead = lax.rem(section + sections - 1, sections)

    def turn(t):
        half = (t + 1) // 2
        step = half + (1 - t % 2) * (peers - 2 * half)
        return lax.rem(me + step, peers)

    barrier = pltpu.get_barrier_semaphore()

    @pl.loop(0, peers)
    def _(t):
        who = turn(t)
        for where in (after, ahead):
            pl.semaphore_signal(
                barrier, inc=1, device_id={"section": where, "peer": who}, device_id_type=MESH
            )

    @pl.loop(1, peers)
    def _(t):
        pl.semaphore_signal(
            barrier, inc=1, device_id={"section": section, "peer": turn(t)}, device_id_type=MESH
        )

    pl.semaphore_wait(barrier, 3 * peers - 1)

    def remote(src, dst, sems, where, who):
        return pltpu.make_async_remote_copy(
            src_ref=src.at[who],
            dst_ref=dst.at[me],
            send_sem=sems.at[0, who],
            recv_sem=sems.at[1, me],
            device_id={"section": where, "peer": who},
            device_id_type=MESH,
        )

    def arrival(src, dst, sems, where, who):
        return pltpu.make_async_remote_copy(
            src_ref=src.at[who],
            dst_ref=dst.at[who],
            send_sem=sems.at[0, who],
            recv_sem=sems.at[1, who],
            device_id={"section": where, "peer": who},
            device_id_type=MESH,
        )

    own = (
        pltpu.make_async_copy(up.at[me], up_got.at[me], own_sem.at[0]),
        pltpu.make_async_copy(down.at[me], down_got.at[me], own_sem.at[1]),
    )
    for copy in own:
        copy.start()

    @pl.loop(1, peers)
    def _(t):
        who = turn(t)
        remote(up, up_got, sems_u, section, who).start()
        remote(down, down_got, sems_d, section, who).start()

    @pl.loop(0, peers)
    def _(t):
        who = turn(t)
        remote(fwd, fwd_out, sems_f, after, who).start()
        remote(back, back_out, sems_b, ahead, who).start()

    for copy in own:
        copy.wait()

    @pl.loop(1, peers)
    def _(t):
        who = turn(t)
        arrival(up, up_got, sems_u, section, who).wait_recv()
        arrival(down, down_got, sems_d, section, who).wait_recv()

    mask = mask_ref[0]

    @pl.loop(0, peers)
    def _(p):
        pair = jnp.bitwise_xor(p, mask)
        up_send[p] = up_got[pair]
        down_send[p] = down_got[pair]

    @pl.loop(1, peers)
    def _(t):
        who = turn(t)
        remote(up_send, up_out, sems_u2, section, who).start()
        remote(down_send, down_out, sems_d2, section, who).start()

    back_home = (
        pltpu.make_async_copy(up_send.at[me], up_out.at[me], own_sem.at[2]),
        pltpu.make_async_copy(down_send.at[me], down_out.at[me], own_sem.at[3]),
    )
    for copy in back_home:
        copy.start()

    @pl.loop(1, peers)
    def _(t):
        who = turn(t)
        remote(up, up_got, sems_u, section, who).wait_send()
        remote(down, down_got, sems_d, section, who).wait_send()

    @pl.loop(0, peers)
    def _(t):
        who = turn(t)
        remote(fwd, fwd_out, sems_f, after, who).wait_send()
        remote(back, back_out, sems_b, ahead, who).wait_send()
        arrival(fwd, fwd_out, sems_f, after, who).wait_recv()
        arrival(back, back_out, sems_b, ahead, who).wait_recv()

    for copy in back_home:
        copy.wait()

    @pl.loop(1, peers)
    def _(t):
        who = turn(t)
        remote(up_send, up_out, sems_u2, section, who).wait_send()
        remote(down_send, down_out, sems_d2, section, who).wait_send()
        arrival(up_send, up_out, sems_u2, section, who).wait_recv()
        arrival(down_send, down_out, sems_d2, section, who).wait_recv()


def exchange(mask, fwd, back, up, down, sections, peers):
    smem = pl.BlockSpec(memory_space=pltpu.SMEM)
    hbm = pl.BlockSpec(memory_space=pl.ANY)
    like = lambda a: jax.ShapeDtypeStruct(a.shape, a.dtype)
    dma = pltpu.SemaphoreType.DMA
    return pl.pallas_call(
        functools.partial(exchange_kernel, sections, peers),
        name="exchange",
        in_specs=[smem, hbm, hbm, hbm, hbm],
        out_specs=[hbm] * 4,
        out_shape=[like(fwd), like(back), like(up), like(down)],
        scratch_shapes=[
            pltpu.VMEM(up.shape, up.dtype),
            pltpu.VMEM(down.shape, down.dtype),
            pltpu.VMEM(up.shape, up.dtype),
            pltpu.VMEM(down.shape, down.dtype),
        ]
        + [dma((2, peers))] * 6
        + [dma((4,))],
        compiler_params=pltpu.CompilerParams(collective_id=0, has_side_effects=True),
    )(mask, fwd, back, up, down)


def settle_kernel(
    fpick, bpick, fwd, back, up, down, up_other, down_other, next_ref, ret_ref, gdown, gup
):
    f32 = jnp.float32
    next_ref[...] = fwd[...]
    ret_ref[...] = back[...]
    gup[...] = (up[...].astype(f32) + up_other[...].astype(f32)) * 0.5
    gdown[...] = (down[...].astype(f32) + down_other[...].astype(f32)) * 0.5


def settle(fpick, bpick, fwd, back, up, down, up_other, down_other):
    blocks, blk, width = up.shape
    deep, rank = down.shape[1:]
    rows_in = lambda pick: (1, blk, width)
    row = pl.BlockSpec((1, blk, width), lambda i, f, b: (i, 0, 0))
    deep_row = pl.BlockSpec((1, deep, rank), lambda i, f, b: (i, 0, 0))
    return pl.pallas_call(
        settle_kernel,
        name="settle",
        grid_spec=pltpu.PrefetchScalarGridSpec(
            num_scalar_prefetch=2,
            grid=(blocks,),
            in_specs=[
                pl.BlockSpec((1, blk, width), lambda i, f, b: (f[i], 0, 0)),
                pl.BlockSpec((1, blk, width), lambda i, f, b: (b[i], 0, 0)),
                row,
                deep_row,
                row,
                deep_row,
            ],
            out_specs=[row, row, deep_row, row],
        ),
        out_shape=[
            jax.ShapeDtypeStruct((blocks, blk, width), fwd.dtype),
            jax.ShapeDtypeStruct((blocks, blk, width), back.dtype),
            jax.ShapeDtypeStruct((blocks, deep, rank), jnp.float32),
            jax.ShapeDtypeStruct((blocks, blk, width), jnp.float32),
        ],
    )(fpick, bpick, fwd, back, up, down, up_other, down_other)


def tables(counts):
    n = counts.shape[0]
    order = jnp.arange(n, dtype=jnp.int32)
    start = jnp.sum(jnp.where(order[None, :] < order[:, None], counts[None, :], 0), axis=1)
    slot = jnp.minimum(start[:, None] + jnp.arange(CAP, dtype=jnp.int32)[None, :], n - 1)
    inside = (order[:, None] >= start[None, :]) & (order[:, None] < (start + counts)[None, :])
    place = order[None, :] * CAP + order[:, None] - start[None, :]
    pick = jnp.sum(jnp.where(inside, place, 0), axis=1)
    return slot.reshape(-1).astype(jnp.int32), pick.astype(jnp.int32)


def body(inputs, out_grad, gains, down_proj, up_proj, wiring, pair_mask):
    sections = lax.axis_size("section")
    peers = lax.axis_size("peer")
    section = lax.axis_index("section")
    peer = lax.axis_index("peer")
    x = inputs[0, 0]
    rows, width = x.shape
    rank = down_proj.shape[2]
    blk = rows // peers
    here = lax.dynamic_slice(wiring, (section, peer, 0), (1, 1, peers)).reshape(peers)
    before = lax.dynamic_slice(
        wiring, (lax.rem(section + sections - 1, sections), 0, peer), (1, peers, 1)
    ).reshape(peers)
    mask = lax.dynamic_slice(pair_mask, (section,), (1,))
    fslot, bpick = tables(here)
    bslot, fpick = tables(before)
    fwd, back, up, down = layer(
        x, out_grad[0, 0], gains, down_proj[0], up_proj[0], fslot, bslot, peers
    )
    up = up.reshape(peers, rank // peers, width)
    down = down.reshape(peers, width // peers, rank)
    shape = (peers, CAP, blk, width)
    got_fwd, got_back, up_other, down_other = exchange(
        mask, fwd.reshape(shape), back.reshape(shape), up, down, sections, peers
    )
    flat = (peers * CAP, blk, width)
    next_rows, return_rows, grad_down, grad_up = settle(
        fpick, bpick, got_fwd.reshape(flat), got_back.reshape(flat), up, down, up_other, down_other
    )
    return (
        next_rows.reshape(1, 1, rows, width),
        return_rows.reshape(1, 1, rows, width),
        grad_down.reshape(1, 1, width, rank),
        grad_up.reshape(1, 1, rank, width),
    )


def solution(mesh):
    placed = (
        P("section", "peer", None, None),
        P("section", "peer", None, None),
        P("section", None),
        P("section", None, None),
        P("section", None, None),
        P(),
        P(),
    )
    return jax.shard_map(
        body,
        mesh=mesh,
        in_specs=placed,
        out_specs=(
            P("section", "peer", None, None),
            P("section", "peer", None, None),
            P("section", "peer", None, None),
            P("section", "peer", None, None),
        ),
        check_vma=False,
    )
```

time: 423 us -> 281 us (0.66)
  the two profiles are of different devices: /device:TPU:14 before, /device:TPU:64 now
where the time goes in v1:
time: 281 us; the launch traced here: 278 us
  Pallas kernels  271 us (96%)
  local copies, waits for them, and re-layouts  4.08 us (1%)
    pallas_call x1, Pallas kernels, exchange(): pl.pallas_call(functools.partial(exchange_kernel, sections, peers), name=...  245 us
    pallas_call x1, Pallas kernels, layer(): pl.pallas_call(layer_kernel, name='adapter', in_specs=[smem, smem, vmem,...  14.4 us
    pallas_call x1, Pallas kernels, settle(): pl.pallas_call(settle_kernel, name='settle', grid_spec=pltpu.PrefetchScal...  12.1 us

profile of v1, /device:TPU:64, one launch (start us, length us, event | category | flops | bytes accessed | tf_op | source)
XLA Modules:
  0.0 277.8 jit_solution(2104035066199439331)
XLA Ops:
  0.6 0.9 dynamic-slice_reduce_fusion
  1.5 1.2 dynamic_slice.11.mask_ref
  2.8 0.7 dynamic-slice_bitcast_fusion
  3.5 0.1 select_reduce_fusion.1
  3.6 0.7 fusion.2
  4.3 0.7 select_reduce_fusion
  5.0 0.1 add_minimum_fusion
  5.0 0.7 min.17.bslot
  5.7 0.1 add_minimum_fusion.1
  5.8 0.6 min.15.fslot
  6.4 14.4 %adapter.1 = (bf16[32,8,5120]{2,1,0:T(8,128)(2,1)}, bf16[32,8,5120]{2,1,0:T(8,128)(2,1)}, bf16[128,5120]{1,0:T(8,128)(2,1)}, bf16[5120,128]{1,0:T(8,128)(2,1)}) custom-call(s32[32]{0:T(128)} %min.15.fslot, s32[32]{0:T(128)} %min.17.bslot, bf16[128,5120]{1,0:T(8,128)(2,1)} %bitcast.26, bf16[128,5120]{1,0:T(8,128)(2,1)} %bitcast.27, f32[1,5120]{1,0:T(1,128)} %g_ref.1, ...), custom_call_target="tpu_custom_call" | custom-call | tf_op jit(solution)/shard_map/adapter/pallas_call | solution.py:106
  20.8 244.8 %exchange.1 = (bf16[16,2,8,5120]{3,2,1,0:T(8,128)(2,1)}, bf16[16,2,8,5120]{3,2,1,0:T(8,128)(2,1)}, bf16[16,8,5120]{2,1,0:T(8,128)(2,1)}, bf16[16,320,128]{2,1,0:T(8,128)(2,1)}) custom-call(s32[1]{0:T(128)} %dynamic_slice.11.mask_ref, bf16[16,2,8,5120]{3,2,1,0:T(8,128)(2,1)} %bitcast.22, bf16[16,2,8,5120]{3,2,1,0:T(8,128)(2,1)} %bitcast.23, ...), custom_call_target="tpu_custom_call" | custom-call | tf_op jit(solution)/shard_map/exchange/pallas_call | solution.py:262
  265.6 12.1 %settle.1 = (bf16[16,8,5120]{2,1,0:T(8,128)(2,1)}, bf16[16,8,5120]{2,1,0:T(8,128)(2,1)}, f32[16,320,128]{2,1,0:T(8,128)}, f32[16,8,5120]{2,1,0:T(8,128)}) custom-call(s32[16]{0:T(128)} %get-tuple-element.29.fpick, s32[16]{0:T(128)} %get-tuple-element.28.bpick, bf16[32,8,5120]{2,1,0:T(8,128)(2,1)} %bitcast.24, bf16[32,8,5120]{2,1,0:T(8,128)(2,1)} %bitcast.25, ...), custom_call_target="tpu_custom_call" | custom-call | tf_op jit(solution)/shard_map/settle/pallas_call | solution.py:296
  (2 shorter events, 0.0 us)

commit v2 on v0

v2 whole, which is shorter than its diff:
```python
import functools

import jax
import jax.numpy as jnp
from jax import lax
from jax.experimental import pallas as pl
from jax.experimental.pallas import tpu as pltpu
from jax.sharding import PartitionSpec as P

CAP = 2
WIDE = 512
PARTS = 4
MESH = pl.DeviceIdType.MESH
F32, BF16 = jnp.float32, jnp.bfloat16


def dims(a, b):
    return (((a,), (b,)), ((), ()))


def section_kernel(
    sections, peers, masks, g_ref, wiring, x_hbm, dy_hbm, down_hbm, up_hbm,
    fwd_out, back_out, gup_out, gdown_out, gup2_out, gdown2_out,
    x_own, dy_own, down_ref, up_ref, x_got, dy_got, x_send, dy_send, x_pair, dy_pair,
    normed, dns, outs, dxs, fwd, back, gup, gdown, gup2, gdown2, counts,
    load_sem, own_sem, out_sem, x1, dy1, x2, dy2, sems_f, sems_b,
):
    section = lax.axis_index("section")
    me = lax.axis_index("peer")
    after = lax.rem(section + 1, sections)
    ahead = lax.rem(section + sections - 1, sections)
    blocks, blk, width = x_own.shape
    rows = blocks * blk
    rank = up_ref.shape[0]
    chunks = width // WIDE

    def turn(t):
        half = (t + 1) // 2
        step = half + (1 - t % 2) * (peers - 2 * half)
        return lax.rem(me + step, peers)

    loads = [
        pltpu.make_async_copy(src, dst, load_sem.at[i])
        for i, (src, dst) in enumerate((
            (x_hbm, x_own),
            (dy_hbm, dy_own),
            (down_hbm, down_ref),
            (up_hbm, up_ref),
            (wiring.at[section], counts.at[0]),
            (wiring.at[ahead], counts.at[1]),
            (x_hbm.at[me], x_got.at[me]),
            (dy_hbm.at[me], dy_got.at[me]),
        ))
    ]
    for copy in loads:
        copy.start()

    barrier = pltpu.get_barrier_semaphore()

    @pl.loop(0, peers)
    def _(t):
        who = turn(t)
        for where in (after, ahead):
            pl.semaphore_signal(
                barrier, inc=1, device_id={"section": where, "peer": who}, device_id_type=MESH
            )

    @pl.loop(1, peers)
    def _(t):
        pl.semaphore_signal(
            barrier, inc=1, device_id={"section": section, "peer": turn(t)}, device_id_type=MESH
        )

    pl.semaphore_wait(barrier, 3 * peers - 1)

    def remote(src, dst, sems, where, who):
        return pltpu.make_async_remote_copy(
            src_ref=src.at[who],
            dst_ref=dst.at[me],
            send_sem=sems.at[0, who],
            recv_sem=sems.at[1, me],
            device_id={"section": where, "peer": who},
            device_id_type=MESH,
        )

    def arrival(src, dst, sems, where, who):
        return pltpu.make_async_remote_copy(
            src_ref=src.at[who],
            dst_ref=dst.at[who],
            send_sem=sems.at[0, who],
            recv_sem=sems.at[1, who],
            device_id={"section": where, "peer": who},
            device_id_type=MESH,
        )

    @pl.loop(1, peers)
    def _(t):
        who = turn(t)
        remote(x_hbm, x_got, x1, section, who).start()
        remote(dy_hbm, dy_got, dy1, section, who).start()

    for copy in loads:
        copy.wait()

    def cols(c):
        return pl.ds(pl.multiple_of(c * WIDE, WIDE), WIDE)

    def wide(ref, at):
        return ref[:, :, at].astype(F32).reshape(rows, WIDE)

    def tall(value):
        return value.reshape(blocks, blk, WIDE).astype(BF16)

    def head(x_ref, dy_ref):
        def squares(c, total):
            xc = wide(x_ref, cols(c))
            return total + jnp.sum(xc * xc, axis=1, keepdims=True)

        ms = lax.fori_loop(0, chunks, squares, jnp.zeros((rows, 1), F32)) / width
        rinv = lax.rsqrt(ms + 1e-05)

        def project(c, carry):
            pre, dact = carry
            at = cols(c)
            nc = (wide(x_ref, at) * rinv * g_ref[:, at]).astype(BF16)
            normed[:, at] = nc
            pre = pre + jnp.dot(nc, down_ref[at, :], preferred_element_type=F32)
            dact = dact + lax.dot_general(
                wide(dy_ref, at).astype(BF16), up_ref[:, at], dims(1, 1), preferred_element_type=F32
            )
            return pre, dact

        zero = jnp.zeros((rows, rank), F32)
        pre, dact = lax.fori_loop(0, chunks, project, (zero, zero))
        sig = jax.nn.sigmoid(pre)
        act = (pre * sig).astype(BF16)
        dpre = (dact * sig * (1.0 + pre * (1.0 - sig))).astype(BF16)
        return rinv, act, dpre

    def gradients(at, dy_ref, act, dpre, up_to, down_to):
        up_to[:, :, at] = tall(
            lax.dot_general(
                act, wide(dy_ref, at).astype(BF16), dims(0, 0), preferred_element_type=F32
            )
        )
        down_to[at, :] = lax.dot_general(
            normed[:, at], dpre, dims(0, 0), preferred_element_type=F32
        ).astype(BF16)

    rinv, act, dpre = head(x_own, dy_own)

    def tail(c, inner):
        at = cols(c)
        xc = wide(x_own, at)
        outs[:, :, at] = tall(xc + jnp.dot(act, up_ref[:, at], preferred_element_type=F32))
        dn = (
            lax.dot_general(dpre, down_ref[at, :], dims(1, 1), preferred_element_type=F32)
            * g_ref[:, at]
        )
        dns[:, at] = dn
        gradients(at, dy_own, act, dpre, gup, gdown)
        return inner + jnp.sum(dn * xc, axis=1, keepdims=True)

    inner = lax.fori_loop(0, chunks, tail, jnp.zeros((rows, 1), F32)) / width
    pull = rinv * rinv * inner

    @pl.loop(0, chunks)
    def _(c):
        at = cols(c)
        dxs[:, :, at] = tall(wide(dy_own, at) + rinv * (dns[:, at] - wide(x_own, at) * pull))

    def spread(source, target, count):
        def one(q, start):
            for slot in range(CAP):
                target[q, slot] = source[jnp.minimum(start + slot, blocks - 1)]
            return start + count(q)

        lax.fori_loop(0, peers, one, jnp.int32(0))

    spread(dxs, back, lambda q: counts[1, q, me])

    @pl.loop(0, peers)
    def _(t):
        remote(back, back_out, sems_b, ahead, turn(t)).start()

    spread(outs, fwd, lambda q: counts[0, me, q])
    saves = [
        pltpu.make_async_copy(gup, gup_out, out_sem.at[0]),
        pltpu.make_async_copy(gdown, gdown_out, out_sem.at[1]),
    ]
    for copy in saves:
        copy.start()

    mask = masks[section]

    @pl.loop(1, peers)
    def _(t):
        who = turn(t)
        arrival(x_hbm, x_got, x1, section, who).wait_recv()
        arrival(dy_hbm, dy_got, dy1, section, who).wait_recv()

    @pl.loop(0, peers)
    def _(p):
        pair = jnp.bitwise_xor(p, mask)
        x_send[p] = x_got[pair]
        dy_send[p] = dy_got[pair]

    @pl.loop(1, peers)
    def _(t):
        who = turn(t)
        remote(x_send, x_pair, x2, section, who).start()
        remote(dy_send, dy_pair, dy2, section, who).start()

    kept = [
        pltpu.make_async_copy(x_send.at[me], x_pair.at[me], own_sem.at[0]),
        pltpu.make_async_copy(dy_send.at[me], dy_pair.at[me], own_sem.at[1]),
    ]
    for copy in kept:
        copy.start()

    @pl.loop(0, peers)
    def _(t):
        remote(fwd, fwd_out, sems_f, after, turn(t)).start()

    for copy in kept:
        copy.wait()

    @pl.loop(1, peers)
    def _(t):
        who = turn(t)
        arrival(x_send, x_pair, x2, section, who).wait_recv()
        arrival(dy_send, dy_pair, dy2, section, who).wait_recv()

    _, act2, dpre2 = head(x_pair, dy_pair)

    @pl.loop(0, chunks)
    def _(c):
        gradients(cols(c), dy_pair, act2, dpre2, gup2, gdown2)

    saves += [
        pltpu.make_async_copy(gup2, gup2_out, out_sem.at[2]),
        pltpu.make_async_copy(gdown2, gdown2_out, out_sem.at[3]),
    ]
    for copy in saves[2:]:
        copy.start()

    @pl.loop(1, peers)
    def _(t):
        who = turn(t)
        remote(x_hbm, x_got, x1, section, who).wait_send()
        remote(dy_hbm, dy_got, dy1, section, who).wait_send()
        remote(x_send, x_pair, x2, section, who).wait_send()
        remote(dy_send, dy_pair, dy2, section, who).wait_send()

    @pl.loop(0, peers)
    def _(t):
        who = turn(t)
        remote(fwd, fwd_out, sems_f, after, who).wait_send()
        remote(back, back_out, sems_b, ahead, who).wait_send()
        arrival(fwd, fwd_out, sems_f, after, who).wait_recv()
        arrival(back, back_out, sems_b, ahead, who).wait_recv()

    for copy in saves:
        copy.wait()


def run_section(masks, g, wiring, x, dy, down, up, sections, peers):
    vmem = pl.BlockSpec(memory_space=pltpu.VMEM)
    smem = pl.BlockSpec(memory_space=pltpu.SMEM)
    hbm = pl.BlockSpec(memory_space=pl.ANY)
    dma = pltpu.SemaphoreType.DMA
    blocks, blk, width = x.shape
    rows, rank = blocks * blk, up.shape[0]
    piece = pltpu.VMEM(x.shape, BF16)
    slots = (peers, CAP, blk, width)
    up3 = (peers, rank // peers, width)
    return pl.pallas_call(
        functools.partial(section_kernel, sections, peers),
        name="section_layer",
        in_specs=[smem, vmem] + [hbm] * 5,
        out_specs=[hbm] * 6,
        out_shape=[
            jax.ShapeDtypeStruct(slots, BF16),
            jax.ShapeDtypeStruct(slots, BF16),
            jax.ShapeDtypeStruct(up3, BF16),
            jax.ShapeDtypeStruct(down.shape, BF16),
            jax.ShapeDtypeStruct(up3, BF16),
            jax.ShapeDtypeStruct(down.shape, BF16),
        ],
        scratch_shapes=[
            piece, piece, pltpu.VMEM(down.shape, BF16), pltpu.VMEM(up.shape, BF16),
            piece, piece, piece, piece, piece, piece,
            pltpu.VMEM((rows, width), BF16), pltpu.VMEM((rows, width), F32),
            piece, piece, pltpu.VMEM(slots, BF16), pltpu.VMEM(slots, BF16),
            pltpu.VMEM(up3, BF16), pltpu.VMEM(down.shape, BF16),
            pltpu.VMEM(up3, BF16), pltpu.VMEM(down.shape, BF16),
            pltpu.SMEM((2, peers, peers), jnp.int32),
            dma((8,)), dma((2,)), dma((4,)),
        ]
        + [dma((2, peers))] * 6,
        compiler_params=pltpu.CompilerParams(
            collective_id=0, has_side_effects=True, vmem_limit_bytes=60 * 1024 * 1024
        ),
    )(masks, g, wiring, x, dy, down, up)


def settle_kernel(
    sections, wiring, fwd, back, up, down, up2, down2,
    next_out, ret_out, gdown_out, gup_out,
    counts, nexts, rets, ups, downs, up2s, down2s, gups, gdowns,
    count_sem, row_sem, read_sem, write_sem,
):
    section = lax.axis_index("section")
    me = lax.axis_index("peer")
    ahead = lax.rem(section + sections - 1, sections)
    tables = [
        pltpu.make_async_copy(wiring.at[section], counts.at[0], count_sem.at[0]),
        pltpu.make_async_copy(wiring.at[ahead], counts.at[1], count_sem.at[1]),
    ]
    for copy in tables:
        copy.start()
    peers = counts.shape[1]

    def part(ref, c):
        size = ref.shape[0] // PARTS
        return ref.at[pl.ds(c * size, size)]

    pairs = ((up, ups), (up2, up2s), (down, downs), (down2, down2s))
    reads = [
        [
            pltpu.make_async_copy(part(src, c), part(dst, c), read_sem.at[c, i])
            for i, (src, dst) in enumerate(pairs)
        ]
        for c in range(PARTS)
    ]
    for copy in reads[0]:
        copy.start()
    for copy in tables:
        copy.wait()

    def gather(p, starts):
        moved = []
        for k, (source, target, n) in enumerate(
            ((fwd, nexts, counts[1, p, me]), (back, rets, counts[0, me, p]))
        ):
            for slot in range(CAP):
                @pl.when(slot < n)
                def _():
                    at = starts[k] + slot
                    pltpu.make_async_copy(
                        source.at[p, slot], target.at[at], row_sem.at[k, at]
                    ).start()

            moved.append(starts[k] + n)
        return tuple(moved)

    lax.fori_loop(0, peers, gather, (jnp.int32(0), jnp.int32(0)))
    for group in reads[1:]:
        for copy in group:
            copy.start()

    writes = []
    for c in range(PARTS):
        for copy in reads[c]:
            copy.wait()
        for a, b, total, out, i in (
            (ups, up2s, gups, gup_out, 0),
            (downs, down2s, gdowns, gdown_out, 1),
        ):
            size = a.shape[0] // PARTS
            at = pl.ds(c * size, size)
            total[at] = (a[at].astype(F32) + b[at].astype(F32)) * 0.5
            writes.append(
                pltpu.make_async_copy(part(total, c), part(out, c), write_sem.at[c, i])
            )
            writes[-1].start()

    for k, (source, target, out) in enumerate(((fwd, nexts, next_out), (back, rets, ret_out))):
        @pl.loop(0, peers)
        def _(b):
            pltpu.make_async_copy(source.at[0, 0], target.at[b], row_sem.at[k, b]).wait()

        writes.append(pltpu.make_async_copy(target, out, write_sem.at[PARTS, k]))
        writes[-1].start()
    for copy in writes:
        copy.wait()


def settle(wiring, fwd, back, up, down, up2, down2, sections):
    hbm = pl.BlockSpec(memory_space=pl.ANY)
    dma = pltpu.SemaphoreType.DMA
    peers, _, blk, width = fwd.shape
    rows = (peers, blk, width)
    return pl.pallas_call(
        functools.partial(settle_kernel, sections),
        name="settle",
        in_specs=[hbm] * 7,
        out_specs=[hbm] * 4,
        out_shape=[
            jax.ShapeDtypeStruct(rows, BF16),
            jax.ShapeDtypeStruct(rows, BF16),
            jax.ShapeDtypeStruct(down.shape, F32),
            jax.ShapeDtypeStruct(up.shape, F32),
        ],
        scratch_shapes=[
            pltpu.SMEM((2, peers, peers), jnp.int32),
            pltpu.VMEM(rows, BF16), pltpu.VMEM(rows, BF16),
            pltpu.VMEM(up.shape, BF16), pltpu.VMEM(down.shape, BF16),
            pltpu.VMEM(up.shape, BF16), pltpu.VMEM(down.shape, BF16),
            pltpu.VMEM(up.shape, F32), pltpu.VMEM(down.shape, F32),
            dma((2,)), dma((2, peers)), dma((PARTS, 4)), dma((PARTS + 1, 2)),
        ],
    )(wiring, fwd, back, up, down, up2, down2)


def body(inputs, out_grad, gains, down_proj, up_proj, wiring, pair_mask):
    sections = lax.axis_size("section")
    peers = lax.axis_size("peer")
    rows, width = inputs.shape[2:]
    rank = down_proj.shape[2]
    pieces = (peers, rows // peers, width)
    fwd, back, up, down, up2, down2 = run_section(
        pair_mask, gains, wiring, inputs.reshape(pieces), out_grad.reshape(pieces),
        down_proj[0], up_proj[0], sections, peers,
    )
    next_rows, return_rows, grad_down, grad_up = settle(
        wiring, fwd, back, up, down, up2, down2, sections
    )
    return (
        next_rows.reshape(1, 1, rows, width),
        return_rows.reshape(1, 1, rows, width),
        grad_down.reshape(1, 1, width, rank),
        grad_up.reshape(1, 1, rank, width),
    )


def solution(mesh):
    placed = (
        P("section", "peer", None, None),
        P("section", "peer", None, None),
        P("section", None),
        P("section", None, None),
        P("section", None, None),
        P(),
        P(),
    )
    return jax.shard_map(
        body,
        mesh=mesh,
        in_specs=placed,
        out_specs=(
            P("section", "peer", None, None),
            P("section", "peer", None, None),
            P("section", "peer", None, None),
            P("section", "peer", None, None),
        ),
        check_vma=False,
    )
```

time: 423 us -> 258 us (0.61)
  the two profiles are of different devices: /device:TPU:14 before, /device:TPU:64 now
where the time goes in v2:
time: 258 us; the launch traced here: 254 us
  Pallas kernels  253 us (98%)
    pallas_call x1, Pallas kernels, run_section(): pl.pallas_call(functools.partial(section_kernel, sections, peers), name='...  246 us
    pallas_call x1, Pallas kernels, settle(): pl.pallas_call(functools.partial(settle_kernel, sections), name='settle',...  7.07 us

profile of v2, /device:TPU:64, one launch (start us, length us, event | category | flops | bytes accessed | tf_op | source)
XLA Modules:
  0.0 253.6 jit_solution(12516174555064761478)
XLA Ops:
  0.6 245.9 %section_layer.1 = (bf16[16,2,8,5120]{3,2,1,0:T(8,128)(2,1)}, bf16[16,2,8,5120]{3,2,1,0:T(8,128)(2,1)}, bf16[16,8,5120]{2,1,0:T(8,128)(2,1)}, bf16[5120,128]{1,0...) custom-call(s32[16]{0:T(128)} %masks.1, f32[1,5120]{1,0:T(1,128)} %g_ref.1, ...), custom_call_target="tpu_custom_call" | custom-call | tf_op jit(solution)/shard_map/section_layer/pallas_call | solution.py:277
  246.5 7.1 %settle.1 = (bf16[16,8,5120]{2,1,0:T(8,128)(2,1)}, bf16[16,8,5120]{2,1,0:T(8,128)(2,1)}, f32[5120,128]{1,0:T(8,128)}, f32[16,8,5120]{2,1,0:T(8,128)}) custom-call(s32[16,16,16]{2,1,0:T(8,128)} %wiring.3, bf16[16,2,8,5120]{3,2,1,0:T(8,128)(2,1)} %get-tuple-element.14.fwd, bf16[16,2,8,5120]{3,2,1,0:T(8,128)(2,1)} %get-tuple-element.15.back, ...), custom_call_target="tpu_custom_call" | custom-call | tf_op jit(solution)/shard_map/settle/pallas_call | solution.py:394

commit v3 on v2

v3 whole, which is shorter than its diff:
```python
import functools

import jax
import jax.numpy as jnp
from jax import lax
from jax.experimental import pallas as pl
from jax.experimental.pallas import tpu as pltpu
from jax.sharding import PartitionSpec as P

CAP = 2
WIDE = 512
PARTS = 4
EARLY = 8
MESH = pl.DeviceIdType.MESH
F32, BF16 = jnp.float32, jnp.bfloat16


def dims(a, b):
    return (((a,), (b,)), ((), ()))


def mul(a, b, ca=1, cb=0):
    return lax.dot_general(a, b, dims(ca, cb), preferred_element_type=F32)


def hot(mask):
    return mask.astype(F32).astype(BF16)


def iota(shape, dim):
    return lax.broadcasted_iota(jnp.int32, shape, dim)


def block_graph(counts):
    n = counts.shape[0]
    e, bits = n * n, n.bit_length() - 1
    c = counts.astype(BF16)
    start = mul(c, hot(iota((n, n), 0) < iota((n, n), 1)))
    above = mul(hot(iota((n, n), 1) < iota((n, n), 0)), c)
    right = hot((iota((e, n), 0) >> bits) == iota((e, n), 1))
    left = hot((iota((n, e), 1) >> bits) == iota((n, e), 0))

    def grow(m):
        return mul(mul(right, m.astype(BF16), 1, 1).astype(BF16), left)

    rank = (iota((e, e), 1) & (n - 1)).astype(F32) - grow(start)
    place = (iota((e, e), 0) & (n - 1)).astype(F32)
    inside = (rank >= 0) & (rank < grow(counts)) & (place == grow(above) + rank)
    return hot(inside)


def halve(graph, left, right, size):
    e = graph.shape[0]
    row, col = iota((e, e), 0), iota((e, e), 1)
    swap = hot((row >> 1 == col >> 1) & (row != col))
    mate = mul(graph, mul(swap, graph).astype(BF16), 0, 0).astype(BF16)
    step = mul(mate, swap).astype(BF16)

    def jump(_, carry):
        low, step = carry
        low = jnp.minimum(low, mul(low.astype(BF16), step))
        return low, mul(step, step).astype(BF16)

    longest = e * size >> (e.bit_length() - 1) // 2 + 1
    low, _ = lax.fori_loop(0, longest.bit_length() - 1, jump, (iota((8, e), 1).astype(F32), step))
    side = (low > mul(low.astype(BF16), swap)).astype(F32)
    at = iota((8, e), 1)
    base = ((at & ~(size - 1)) + ((at & (size - 1)) >> 1)).astype(F32)

    def moved(half):
        return hot(row.astype(F32) == (base + half * (size // 2))[0:1, :])

    on_left, on_right = moved(side), moved(mul(side.astype(BF16), graph, 1, 1))
    graph = mul(mul(on_right, graph).astype(BF16), on_left, 1, 1).astype(BF16)
    return graph, mul(on_left, left).astype(BF16), mul(on_right, right).astype(BF16)


def colours(counts):
    graph = block_graph(counts)
    size, e = counts.shape[0], graph.shape[0]
    left = right = hot(iota((e, e), 0) == iota((e, e), 1))
    while size > 1:
        graph, left, right = halve(graph, left, right, size)
        size //= 2
    return graph, left, right


def cut(matrix, blocks, blk, rows_at, cols_at):
    e, n, bits = matrix.shape[0], blocks * blk, blk.bit_length() - 1
    pick = hot(iota((n, e), 1) == rows_at(iota((n, e), 0) >> bits))
    take = hot(iota((e, n), 0) == cols_at(iota((e, n), 1) >> bits))
    found = mul(mul(pick, matrix).astype(BF16), take)
    same = (iota((n, n), 0) & (blk - 1)) == (iota((n, n), 1) & (blk - 1))
    return hot(same & (found > 0.5))


def section_kernel(
    sections, peers, masks, g_ref, wiring, x_hbm, dy_hbm, down_hbm, up_hbm,
    fwd_out, back_out, gup_out, gdown_out, gup2_out, gdown2_out, place_out,
    x_own, dy_own, down_ref, up_ref, x_pack, x_got, dy_got, x_send, dy_send, x_pair, dy_pair,
    x_flat, normed, dns, dxs, fwd, back, gup, gdown, gup2, gdown2, graph_ref, left_ref,
    counts, tables, load_sem, own_sem, out_sem, x1, dy1, x2, dy2, sems_f, sems_b,
):
    section = lax.axis_index("section")
    me = lax.axis_index("peer")
    after = lax.rem(section + 1, sections)
    ahead = lax.rem(section + sections - 1, sections)
    blocks, blk, width = x_own.shape
    rows = blocks * blk
    rank = up_ref.shape[0]
    chunks = width // WIDE

    def turn(t):
        half = (t + 1) // 2
        step = half + (1 - t % 2) * (peers - 2 * half)
        return lax.rem(me + step, peers)

    loads = [
        pltpu.make_async_copy(src, dst, load_sem.at[i])
        for i, (src, dst) in enumerate((
            (x_hbm, x_own),
            (dy_hbm, dy_own),
            (down_hbm, down_ref),
            (up_hbm, up_ref),
            (wiring.at[ahead], counts),
            (wiring.at[section], tables.at[0]),
            (wiring.at[ahead], tables.at[1]),
            (dy_hbm.at[me], dy_got.at[me]),
        ))
    ]
    for copy in loads:
        copy.start()

    barrier = pltpu.get_barrier_semaphore()

    @pl.loop(0, peers)
    def _(t):
        who = turn(t)
        for where in (after, ahead):
            pl.semaphore_signal(
                barrier, inc=1, device_id={"section": where, "peer": who}, device_id_type=MESH
            )

    @pl.loop(1, peers)
    def _(t):
        pl.semaphore_signal(
            barrier, inc=1, device_id={"section": section, "peer": turn(t)}, device_id_type=MESH
        )

    pl.semaphore_wait(barrier, 3 * peers - 1)

    def remote(src, dst, sems, where, who):
        return pltpu.make_async_remote_copy(
            src_ref=src.at[who],
            dst_ref=dst.at[me],
            send_sem=sems.at[0, who],
            recv_sem=sems.at[1, me],
            device_id={"section": where, "peer": who},
            device_id_type=MESH,
        )

    def arrival(src, dst, sems, where, who):
        return pltpu.make_async_remote_copy(
            src_ref=src.at[who],
            dst_ref=dst.at[who],
            send_sem=sems.at[0, who],
            recv_sem=sems.at[1, who],
            device_id={"section": where, "peer": who},
            device_id_type=MESH,
        )

    @pl.loop(1, peers)
    def _(t):
        remote(dy_hbm, dy_got, dy1, section, turn(t)).start()

    for copy in loads:
        copy.wait()

    def cols(c):
        return pl.ds(pl.multiple_of(c * WIDE, WIDE), WIDE)

    def wide(ref, at):
        return ref[:, :, at].astype(F32).reshape(rows, WIDE)

    def tall(value):
        return value.reshape(blocks, blk, WIDE).astype(BF16)

    def inverse(x_ref):
        def squares(c, total):
            xc = wide(x_ref, cols(c))
            return total + jnp.sum(xc * xc, axis=1, keepdims=True)

        ms = lax.fori_loop(0, chunks, squares, jnp.zeros((rows, 1), F32)) / width
        return lax.rsqrt(ms + 1e-05)

    def project(x_ref, rinv, at):
        nc = (wide(x_ref, at) * rinv * g_ref[:, at]).astype(BF16)
        return nc, jnp.dot(nc, down_ref[at, :], preferred_element_type=F32)

    zero = jnp.zeros((rows, rank), F32)

    def head(x_ref, dy_ref):
        rinv = inverse(x_ref)

        def both(c, carry):
            pre, dact = carry
            at = cols(c)
            nc, part = project(x_ref, rinv, at)
            normed[:, at] = nc
            dact = dact + mul(wide(dy_ref, at).astype(BF16), up_ref[:, at], 1, 1)
            return pre + part, dact

        pre, dact = lax.fori_loop(0, chunks, both, (zero, zero))
        sig = jax.nn.sigmoid(pre)
        act = (pre * sig).astype(BF16)
        dpre = (dact * sig * (1.0 + pre * (1.0 - sig))).astype(BF16)
        return rinv, act, dpre

    def gradients(at, dy_ref, act, dpre, up_to, down_to):
        up_to[:, :, at] = tall(mul(act, wide(dy_ref, at).astype(BF16), 0, 0))
        down_to[at, :] = mul(normed[:, at], dpre, 0, 0).astype(BF16)

    rinv, act, dpre = head(x_own, dy_own)

    def tail(c, inner):
        at = cols(c)
        dn = mul(dpre, down_ref[at, :], 1, 1) * g_ref[:, at]
        dns[:, at] = dn
        return inner + jnp.sum(dn * wide(x_own, at), axis=1, keepdims=True)

    inner = lax.fori_loop(0, chunks, tail, jnp.zeros((rows, 1), F32)) / width
    pull = rinv * rinv * inner

    @pl.loop(0, chunks)
    def _(c):
        at = cols(c)
        dxs[:, :, at] = tall(wide(dy_own, at) + rinv * (dns[:, at] - wide(x_own, at) * pull))

    def spread(q, start):
        for slot in range(CAP):
            back[q, slot] = dxs[jnp.minimum(start + slot, blocks - 1)]
        return start + counts[q, me]

    lax.fori_loop(0, peers, spread, jnp.int32(0))

    @pl.loop(0, EARLY)
    def _(t):
        remote(back, back_out, sems_b, ahead, turn(t)).start()

    @pl.loop(0, chunks)
    def _(c):
        gradients(cols(c), dy_own, act, dpre, gup, gdown)

    saves = [
        pltpu.make_async_copy(gup, gup_out, out_sem.at[0]),
        pltpu.make_async_copy(gdown, gdown_out, out_sem.at[1]),
    ]
    for copy in saves:
        copy.start()

    mask = masks[section]
    graph, left, _ = colours(tables[0].astype(F32))
    graph_ref[...] = graph
    left_ref[...] = left

    def order(peer):
        return cut(
            left_ref[...], blocks, blk, lambda k: peer * peers + k, lambda b: peer * peers + b
        )

    mine = order(me)

    @pl.loop(0, chunks)
    def _(c):
        at = cols(c)
        x_pack[:, :, at] = tall(mul(mine, wide(x_own, at).astype(BF16)))

    x_got[me] = x_pack[me]

    @pl.loop(1, peers)
    def _(t):
        remote(x_pack, x_got, x1, section, turn(t)).start()

    @pl.loop(EARLY, peers)
    def _(t):
        remote(back, back_out, sems_b, ahead, turn(t)).start()

    @pl.loop(1, peers)
    def _(t):
        arrival(dy_hbm, dy_got, dy1, section, turn(t)).wait_recv()

    @pl.loop(0, peers)
    def _(p):
        dy_send[p] = dy_got[jnp.bitwise_xor(p, mask)]

    dy_pair[me] = dy_send[me]

    @pl.loop(1, peers)
    def _(t):
        remote(dy_send, dy_pair, dy2, section, turn(t)).start()

    _, _, right = colours(tables[1].astype(F32))
    e = right.shape[0]
    spots = iota((8, e), 1) - me * peers
    value = jnp.where((spots >= 0) & (spots < peers), spots, 0).astype(F32)
    found = mul(value.astype(BF16), right).astype(BF16)
    lanes = place_out.shape[1]
    near = hot(iota((e, lanes), 0) - me * peers == iota((e, lanes), 1))
    place_out[...] = (mul(found, near) + 0.5).astype(jnp.int32)

    @pl.loop(1, peers)
    def _(t):
        arrival(x_pack, x_got, x1, section, turn(t)).wait_recv()

    @pl.loop(0, peers)
    def _(p):
        x_send[p] = x_got[jnp.bitwise_xor(p, mask)]

    x_pair[me] = x_send[me]

    @pl.loop(1, peers)
    def _(t):
        remote(x_send, x_pair, x2, section, turn(t)).start()

    rinv_got = inverse(x_got)
    pre_got = lax.fori_loop(
        0, chunks, lambda c, pre: pre + project(x_got, rinv_got, cols(c))[1], zero
    )
    act_got = (pre_got * jax.nn.sigmoid(pre_got)).astype(BF16)
    sorting = cut(
        graph_ref[...], blocks, blk, lambda q: q * peers + me, lambda p: p * peers + me
    )

    @pl.loop(0, chunks)
    def _(c):
        at = cols(c)
        oc = (wide(x_got, at) + mul(act_got, up_ref[:, at])).astype(BF16)
        fwd[:, :, at] = tall(mul(sorting, oc))

    @pl.loop(0, peers)
    def _(t):
        remote(fwd, fwd_out, sems_f, after, turn(t)).start()

    theirs = order(jnp.bitwise_xor(me, mask))

    @pl.loop(1, peers)
    def _(t):
        who = turn(t)
        arrival(dy_send, dy_pair, dy2, section, who).wait_recv()
        arrival(x_send, x_pair, x2, section, who).wait_recv()

    @pl.loop(0, chunks)
    def _(c):
        at = cols(c)
        x_flat[:, :, at] = tall(mul(theirs, wide(x_pair, at).astype(BF16), 0, 0))

    _, act2, dpre2 = head(x_flat, dy_pair)

    @pl.loop(0, chunks)
    def _(c):
        gradients(cols(c), dy_pair, act2, dpre2, gup2, gdown2)

    saves += [
        pltpu.make_async_copy(gup2, gup2_out, out_sem.at[2]),
        pltpu.make_async_copy(gdown2, gdown2_out, out_sem.at[3]),
    ]
    for copy in saves[2:]:
        copy.start()

    @pl.loop(1, peers)
    def _(t):
        who = turn(t)
        remote(dy_hbm, dy_got, dy1, section, who).wait_send()
        remote(x_pack, x_got, x1, section, who).wait_send()
        remote(dy_send, dy_pair, dy2, section, who).wait_send()
        remote(x_send, x_pair, x2, section, who).wait_send()

    @pl.loop(0, peers)
    def _(t):
        who = turn(t)
        remote(fwd, fwd_out, sems_f, after, who).wait_send()
        remote(back, back_out, sems_b, ahead, who).wait_send()
        arrival(back, back_out, sems_b, ahead, who).wait_recv()
        arrival(fwd, fwd_out, sems_f, after, who).wait_recv()

    for copy in saves:
        copy.wait()


def run_section(masks, g, wiring, x, dy, down, up, sections, peers):
    vmem = pl.BlockSpec(memory_space=pltpu.VMEM)
    smem = pl.BlockSpec(memory_space=pltpu.SMEM)
    hbm = pl.BlockSpec(memory_space=pl.ANY)
    dma = pltpu.SemaphoreType.DMA
    blocks, blk, width = x.shape
    rows, rank = blocks * blk, up.shape[0]
    piece = pltpu.VMEM(x.shape, BF16)
    slots = (peers, CAP, blk, width)
    up3 = (peers, rank // peers, width)
    ups, downs = pltpu.VMEM(up3, BF16), pltpu.VMEM(down.shape, BF16)
    links = pltpu.VMEM((peers * blocks, peers * blocks), BF16)
    return pl.pallas_call(
        functools.partial(section_kernel, sections, peers),
        name="section_layer",
        in_specs=[smem, vmem] + [hbm] * 5,
        out_specs=[hbm] * 6 + [vmem],
        out_shape=[
            jax.ShapeDtypeStruct(x.shape, BF16),
            jax.ShapeDtypeStruct(slots, BF16),
            jax.ShapeDtypeStruct(up3, BF16),
            jax.ShapeDtypeStruct(down.shape, BF16),
            jax.ShapeDtypeStruct(up3, BF16),
            jax.ShapeDtypeStruct(down.shape, BF16),
            jax.ShapeDtypeStruct((8, 128), jnp.int32),
        ],
        scratch_shapes=[piece, piece, downs, pltpu.VMEM(up.shape, BF16)]
        + [piece] * 8
        + [
            pltpu.VMEM((rows, width), BF16), pltpu.VMEM((rows, width), F32),
            piece, piece, pltpu.VMEM(slots, BF16),
            ups, downs, ups, downs, links, links,
            pltpu.SMEM((peers, peers), jnp.int32),
            pltpu.VMEM((2, peers, peers), jnp.int32),
            dma((8,)), dma((2,)), dma((4,)),
        ]
        + [dma((2, peers))] * 6,
        compiler_params=pltpu.CompilerParams(
            collective_id=0, has_side_effects=True, vmem_limit_bytes=60 * 1024 * 1024
        ),
    )(masks, g, wiring, x, dy, down, up)


def settle_kernel(
    wiring, place, fwd, back, up, down, up2, down2,
    next_out, ret_out, gdown_out, gup_out,
    counts, places, nexts, rets, ups, downs, up2s, down2s, gups, gdowns,
    count_sem, row_sem, read_sem, write_sem,
):
    section = lax.axis_index("section")
    me = lax.axis_index("peer")
    tables = [
        pltpu.make_async_copy(wiring.at[section], counts, count_sem.at[0]),
        pltpu.make_async_copy(place, places, count_sem.at[1]),
    ]
    for copy in tables:
        copy.start()
    peers = counts.shape[0]

    def part(ref, c):
        size = ref.shape[0] // PARTS
        return ref.at[pl.ds(c * size, size)]

    pairs = ((up, ups), (up2, up2s), (down, downs), (down2, down2s))
    reads = [
        [
            pltpu.make_async_copy(part(src, c), part(dst, c), read_sem.at[c, i])
            for i, (src, dst) in enumerate(pairs)
        ]
        for c in range(PARTS)
    ]
    for copy in reads[0]:
        copy.start()
    for copy in tables:
        copy.wait()

    def gather(p, start):
        pltpu.make_async_copy(fwd.at[places[0, p]], nexts.at[p], row_sem.at[0, p]).start()
        n = counts[me, p]
        for slot in range(CAP):
            @pl.when(slot < n)
            def _():
                at = start + slot
                pltpu.make_async_copy(back.at[p, slot], rets.at[at], row_sem.at[1, at]).start()

        return start + n

    lax.fori_loop(0, peers, gather, jnp.int32(0))
    for group in reads[1:]:
        for copy in group:
            copy.start()

    writes = []
    for c in range(PARTS):
        for copy in reads[c]:
            copy.wait()
        for a, b, total, out, i in (
            (ups, up2s, gups, gup_out, 0),
            (downs, down2s, gdowns, gdown_out, 1),
        ):
            size = a.shape[0] // PARTS
            at = pl.ds(c * size, size)
            total[at] = (a[at].astype(F32) + b[at].astype(F32)) * 0.5
            writes.append(
                pltpu.make_async_copy(part(total, c), part(out, c), write_sem.at[c, i])
            )
            writes[-1].start()

    for k, (source, target, out) in enumerate(
        ((fwd.at[0], nexts, next_out), (back.at[0, 0], rets, ret_out))
    ):
        @pl.loop(0, peers)
        def _(b):
            pltpu.make_async_copy(source, target.at[b], row_sem.at[k, b]).wait()

        writes.append(pltpu.make_async_copy(target, out, write_sem.at[PARTS, k]))
        writes[-1].start()
    for copy in writes:
        copy.wait()


def settle(wiring, place, fwd, back, up, down, up2, down2):
    hbm = pl.BlockSpec(memory_space=pl.ANY)
    dma = pltpu.SemaphoreType.DMA
    peers, blk, width = fwd.shape
    rows = (peers, blk, width)
    return pl.pallas_call(
        settle_kernel,
        name="settle",
        in_specs=[hbm] * 8,
        out_specs=[hbm] * 4,
        out_shape=[
            jax.ShapeDtypeStruct(rows, BF16),
            jax.ShapeDtypeStruct(rows, BF16),
            jax.ShapeDtypeStruct(down.shape, F32),
            jax.ShapeDtypeStruct(up.shape, F32),
        ],
        scratch_shapes=[
            pltpu.SMEM((peers, peers), jnp.int32),
            pltpu.SMEM(place.shape, jnp.int32),
            pltpu.VMEM(rows, BF16), pltpu.VMEM(rows, BF16),
            pltpu.VMEM(up.shape, BF16), pltpu.VMEM(down.shape, BF16),
            pltpu.VMEM(up.shape, BF16), pltpu.VMEM(down.shape, BF16),
            pltpu.VMEM(up.shape, F32), pltpu.VMEM(down.shape, F32),
            dma((2,)), dma((2, peers)), dma((PARTS, 4)), dma((PARTS + 1, 2)),
        ],
    )(wiring, place, fwd, back, up, down, up2, down2)


def body(inputs, out_grad, gains, down_proj, up_proj, wiring, pair_mask):
    sections = lax.axis_size("section")
    peers = lax.axis_size("peer")
    rows, width = inputs.shape[2:]
    rank = down_proj.shape[2]
    pieces = (peers, rows // peers, width)
    fwd, back, up, down, up2, down2, place = run_section(
        pair_mask, gains, wiring, inputs.reshape(pieces), out_grad.reshape(pieces),
        down_proj[0], up_proj[0], sections, peers,
    )
    next_rows, return_rows, grad_down, grad_up = settle(
        wiring, place, fwd, back, up, down, up2, down2
    )
    return (
        next_rows.reshape(1, 1, rows, width),
        return_rows.reshape(1, 1, rows, width),
        grad_down.reshape(1, 1, width, rank),
        grad_up.reshape(1, 1, rank, width),
    )


def solution(mesh):
    placed = (
        P("section", "peer", None, None),
        P("section", "peer", None, None),
        P("section", None),
        P("section", None, None),
        P("section", None, None),
        P(),
        P(),
    )
    return jax.shard_map(
        body,
        mesh=mesh,
        in_specs=placed,
        out_specs=(
            P("section", "peer", None, None),
            P("section", "peer", None, None),
            P("section", "peer", None, None),
            P("section", "peer", None, None),
        ),
        check_vma=False,
    )
```

time: 258 us -> 224 us (0.87); the launches traced: 254 us -> 222 us
  Pallas kernels: 253 us -> 222 us
    pallas_call x1, Pallas kernels: 246 us -> 215 us  [run_section(): pl.pallas_call(functools.partial(section_kernel, sections, peers), name='...]
where the time goes in v3:
time: 224 us; the launch traced here: 222 us
  Pallas kernels  222 us (99%)
    pallas_call x1, Pallas kernels, run_section(): pl.pallas_call(functools.partial(section_kernel, sections, peers), name='...  215 us
    pallas_call x1, Pallas kernels, settle(): pl.pallas_call(settle_kernel, name='settle', in_specs=[hbm] * 8, out_spec...  6.98 us

profile of v3, /device:TPU:64, one launch (start us, length us, event | category | flops | bytes accessed | tf_op | source)
XLA Modules:
  0.0 222.4 jit_solution(6596928815060385815)
XLA Ops:
  0.6 214.8 %section_layer.1 = (bf16[16,8,5120]{2,1,0:T(8,128)(2,1)}, bf16[16,2,8,5120]{3,2,1,0:T(8,128)(2,1)}, bf16[16,8,5120]{2,1,0:T(8,128)(2,1)}, bf16[5120,128]{1,0:T(8...) custom-call(s32[16]{0:T(128)} %masks.1, f32[1,5120]{1,0:T(1,128)} %g_ref.1, ...), custom_call_target="tpu_custom_call" | custom-call | tf_op jit(solution)/shard_map/section_layer/pallas_call | solution.py:402
  215.4 7.0 %settle.1 = (bf16[16,8,5120]{2,1,0:T(8,128)(2,1)}, bf16[16,8,5120]{2,1,0:T(8,128)(2,1)}, f32[5120,128]{1,0:T(8,128)}, f32[16,8,5120]{2,1,0:T(8,128)}) custom-call(s32[16,16,16]{2,1,0:T(8,128)} %wiring.3, s32[8,128]{1,0:T(8,128)} %get-tuple-element.15.place, bf16[16,8,5120]{2,1,0:T(8,128)(2,1)} %get-tuple-element.16.fwd, ...), custom_call_target="tpu_custom_call" | custom-call | tf_op jit(solution)/shard_map/settle/pallas_call | solution.py:516

commit v4 on v3

--- a/solution.py
+++ b/solution.py
@@ -9,7 +9,6 @@
 
 CAP = 2
 WIDE = 512
-PARTS = 4
 EARLY = 8
 MESH = pl.DeviceIdType.MESH
 F32, BF16 = jnp.float32, jnp.bfloat16
@@ -96,10 +95,10 @@
 
 def section_kernel(
     sections, peers, masks, g_ref, wiring, x_hbm, dy_hbm, down_hbm, up_hbm,
-    fwd_out, back_out, gup_out, gdown_out, gup2_out, gdown2_out, place_out,
+    fwd_out, back_out, gup_out, gdown_out, place_out,
     x_own, dy_own, down_ref, up_ref, x_pack, x_got, dy_got, x_send, dy_send, x_pair, dy_pair,
-    x_flat, normed, dns, dxs, fwd, back, gup, gdown, gup2, gdown2, graph_ref, left_ref,
-    counts, tables, load_sem, own_sem, out_sem, x1, dy1, x2, dy2, sems_f, sems_b,
+    x_flat, normed, dns, dxs, fwd, back, gup, gdown, graph_ref, left_ref,
+    counts, tables, load_sem, x1, dy1, x2, dy2, sems_f, sems_b,
 ):
     section = lax.axis_index("section")
     me = lax.axis_index("peer")
@@ -216,9 +215,9 @@
         dpre = (dact * sig * (1.0 + pre * (1.0 - sig))).astype(BF16)
         return rinv, act, dpre
 
-    def gradients(at, dy_ref, act, dpre, up_to, down_to):
-        up_to[:, :, at] = tall(mul(act, wide(dy_ref, at).astype(BF16), 0, 0))
-        down_to[at, :] = mul(normed[:, at], dpre, 0, 0).astype(BF16)
+    def gradients(at, dy_ref, act, dpre):
+        up_part = tall(mul(act, wide(dy_ref, at).astype(BF16), 0, 0))
+        return up_part, mul(normed[:, at], dpre, 0, 0).astype(BF16)
 
     rinv, act, dpre = head(x_own, dy_own)
 
@@ -249,14 +248,8 @@
 
     @pl.loop(0, chunks)
     def _(c):
-        gradients(cols(c), dy_own, act, dpre, gup, gdown)
-
-    saves = [
-        pltpu.make_async_copy(gup, gup_out, out_sem.at[0]),
-        pltpu.make_async_copy(gdown, gdown_out, out_sem.at[1]),
-    ]
-    for copy in saves:
-        copy.start()
+        at = cols(c)
+        gup[:, :, at], gdown[at, :] = gradients(at, dy_own, act, dpre)
 
     mask = masks[section]
     graph, left, _ = colours(tables[0].astype(F32))
@@ -358,14 +351,10 @@
 
     @pl.loop(0, chunks)
     def _(c):
-        gradients(cols(c), dy_pair, act2, dpre2, gup2, gdown2)
-
-    saves += [
-        pltpu.make_async_copy(gup2, gup2_out, out_sem.at[2]),
-        pltpu.make_async_copy(gdown2, gdown2_out, out_sem.at[3]),
-    ]
-    for copy in saves[2:]:
-        copy.start()
+        at = cols(c)
+        up_part, down_part = gradients(at, dy_pair, act2, dpre2)
+        gup_out[:, :, at] = (gup[:, :, at].astype(F32) + up_part.astype(F32)) * 0.5
+        gdown_out[at, :] = (gdown[at, :].astype(F32) + down_part.astype(F32)) * 0.5
 
     @pl.loop(1, peers)
     def _(t):
@@ -382,9 +371,6 @@
         remote(back, back_out, sems_b, ahead, who).wait_send()
         arrival(back, back_out, sems_b, ahead, who).wait_recv()
         arrival(fwd, fwd_out, sems_f, after, who).wait_recv()
-
-    for copy in saves:
-        copy.wait()
 
 
 def run_section(masks, g, wiring, x, dy, down, up, sections, peers):
@@ -403,137 +389,95 @@
         functools.partial(section_kernel, sections, peers),
         name="section_layer",
         in_specs=[smem, vmem] + [hbm] * 5,
-        out_specs=[hbm] * 6 + [vmem],
+        out_specs=[vmem] * 5,
         out_shape=[
-            jax.ShapeDtypeStruct(x.shape, BF16),
-            jax.ShapeDtypeStruct(slots, BF16),
-            jax.ShapeDtypeStruct(up3, BF16),
-            jax.ShapeDtypeStruct(down.shape, BF16),
-            jax.ShapeDtypeStruct(up3, BF16),
-            jax.ShapeDtypeStruct(down.shape, BF16),
-            jax.ShapeDtypeStruct((8, 128), jnp.int32),
+            pltpu.VMEM(x.shape, BF16),
+            pltpu.VMEM(slots, BF16),
+            pltpu.VMEM(up3, F32),
+            pltpu.VMEM(down.shape, F32),
+            pltpu.VMEM((8, 128), jnp.int32),
         ],
         scratch_shapes=[piece, piece, downs, pltpu.VMEM(up.shape, BF16)]
         + [piece] * 8
         + [
             pltpu.VMEM((rows, width), BF16), pltpu.VMEM((rows, width), F32),
             piece, piece, pltpu.VMEM(slots, BF16),
-            ups, downs, ups, downs, links, links,
+            ups, downs, links, links,
             pltpu.SMEM((peers, peers), jnp.int32),
             pltpu.VMEM((2, peers, peers), jnp.int32),
-            dma((8,)), dma((2,)), dma((4,)),
+            dma((8,)),
         ]
         + [dma((2, peers))] * 6,
         compiler_params=pltpu.CompilerParams(
-            collective_id=0, has_side_effects=True, vmem_limit_bytes=60 * 1024 * 1024
+            collective_id=0, has_side_effects=True, vmem_limit_bytes=48 * 1024 * 1024
         ),
     )(masks, g, wiring, x, dy, down, up)
 
 
 def settle_kernel(
-    wiring, place, fwd, back, up, down, up2, down2,
-    next_out, ret_out, gdown_out, gup_out,
-    counts, places, nexts, rets, ups, downs, up2s, down2s, gups, gdowns,
-    count_sem, row_sem, read_sem, write_sem,
+    wiring, place, fwd, back, up, down, next_out, ret_out, gdown_out, gup_out,
+    counts, places, count_sem, row_sem, sum_sem,
 ):
-    section = lax.axis_index("section")
     me = lax.axis_index("peer")
+    peers = counts.shape[0]
     tables = [
-        pltpu.make_async_copy(wiring.at[section], counts, count_sem.at[0]),
+        pltpu.make_async_copy(wiring.at[lax.axis_index("section")], counts, count_sem.at[0]),
         pltpu.make_async_copy(place, places, count_sem.at[1]),
     ]
-    for copy in tables:
-        copy.start()
-    peers = counts.shape[0]
-
-    def part(ref, c):
-        size = ref.shape[0] // PARTS
-        return ref.at[pl.ds(c * size, size)]
-
-    pairs = ((up, ups), (up2, up2s), (down, downs), (down2, down2s))
-    reads = [
-        [
-            pltpu.make_async_copy(part(src, c), part(dst, c), read_sem.at[c, i])
-            for i, (src, dst) in enumerate(pairs)
-        ]
-        for c in range(PARTS)
+    sums = [
+        pltpu.make_async_copy(up, gup_out, sum_sem.at[0]),
+        pltpu.make_async_copy(down, gdown_out, sum_sem.at[1]),
     ]
-    for copy in reads[0]:
+    for copy in tables + sums:
         copy.start()
     for copy in tables:
         copy.wait()
 
     def gather(p, start):
-        pltpu.make_async_copy(fwd.at[places[0, p]], nexts.at[p], row_sem.at[0, p]).start()
+        pltpu.make_async_copy(fwd.at[places[0, p]], next_out.at[p], row_sem.at[0, p]).start()
         n = counts[me, p]
         for slot in range(CAP):
             @pl.when(slot < n)
             def _():
                 at = start + slot
-                pltpu.make_async_copy(back.at[p, slot], rets.at[at], row_sem.at[1, at]).start()
+                pltpu.make_async_copy(back.at[p, slot], ret_out.at[at], row_sem.at[1, at]).start()
 
         return start + n
 
     lax.fori_loop(0, peers, gather, jnp.int32(0))
-    for group in reads[1:]:
-        for copy in group:
-            copy.start()
-
-    writes = []
-    for c in range(PARTS):
-        for copy in reads[c]:
-            copy.wait()
-        for a, b, total, out, i in (
-            (ups, up2s, gups, gup_out, 0),
-            (downs, down2s, gdowns, gdown_out, 1),
-        ):
-            size = a.shape[0] // PARTS
-            at = pl.ds(c * size, size)
-            total[at] = (a[at].astype(F32) + b[at].astype(F32)) * 0.5
-            writes.append(
-                pltpu.make_async_copy(part(total, c), part(out, c), write_sem.at[c, i])
-            )
-            writes[-1].start()
-
-    for k, (source, target, out) in enumerate(
-        ((fwd.at[0], nexts, next_out), (back.at[0, 0], rets, ret_out))
-    ):
-        @pl.loop(0, peers)
-        def _(b):
-            pltpu.make_async_copy(source, target.at[b], row_sem.at[k, b]).wait()
-
-        writes.append(pltpu.make_async_copy(target, out, write_sem.at[PARTS, k]))
-        writes[-1].start()
-    for copy in writes:
+
+    @pl.loop(0, peers)
+    def _(p):
+        pltpu.make_async_copy(fwd.at[p], next_out.at[p], row_sem.at[0, p]).wait()
+        pltpu.make_async_copy(back.at[p, 0], ret_out.at[p], row_sem.at[1, p]).wait()
+
+    for copy in sums:
         copy.wait()
 
 
-def settle(wiring, place, fwd, back, up, down, up2, down2):
+def settle(wiring, place, fwd, back, up, down):
     hbm = pl.BlockSpec(memory_space=pl.ANY)
+    vmem = pl.BlockSpec(memory_space=pltpu.VMEM)
     dma = pltpu.SemaphoreType.DMA
-    peers, blk, width = fwd.shape
-    rows = (peers, blk, width)
+    peers = fwd.shape[0]
     return pl.pallas_call(
         settle_kernel,
         name="settle",
-        in_specs=[hbm] * 8,
+        in_specs=[hbm] + [vmem] * 5,
         out_specs=[hbm] * 4,
         out_shape=[
-            jax.ShapeDtypeStruct(rows, BF16),
-            jax.ShapeDtypeStruct(rows, BF16),
+            jax.ShapeDtypeStruct(fwd.shape, BF16),
+            jax.ShapeDtypeStruct(fwd.shape, BF16),
             jax.ShapeDtypeStruct(down.shape, F32),
             jax.ShapeDtypeStruct(up.shape, F32),
         ],
         scratch_shapes=[
             pltpu.SMEM((peers, peers), jnp.int32),
             pltpu.SMEM(place.shape, jnp.int32),
-            pltpu.VMEM(rows, BF16), pltpu.VMEM(rows, BF16),
-            pltpu.VMEM(up.shape, BF16), pltpu.VMEM(down.shape, BF16),
-            pltpu.VMEM(up.shape, BF16), pltpu.VMEM(down.shape, BF16),
-            pltpu.VMEM(up.shape, F32), pltpu.VMEM(down.shape, F32),
-            dma((2,)), dma((2, peers)), dma((PARTS, 4)), dma((PARTS + 1, 2)),
+            dma((2,)), dma((2, peers)), dma((2,)),
         ],
-    )(wiring, place, fwd, back, up, down, up2, down2)
+        compiler_params=pltpu.CompilerParams(vmem_limit_bytes=16 * 1024 * 1024),
+    )(wiring, *(pltpu.with_memory_space_constraint(a, pltpu.VMEM) for a in (place, fwd, back, up, down)))
 
 
 def body(inputs, out_grad, gains, down_proj, up_proj, wiring, pair_mask):
@@ -542,13 +486,11 @@
     rows, width = inputs.shape[2:]
     rank = down_proj.shape[2]
     pieces = (peers, rows // peers, width)
-    fwd, back, up, down, up2, down2, place = run_section(
+    fwd, back, up, down, place = run_section(
         pair_mask, gains, wiring, inputs.reshape(pieces), out_grad.reshape(pieces),
         down_proj[0], up_proj[0], sections, peers,
     )
-    next_rows, return_rows, grad_down, grad_up = settle(
-        wiring, place, fwd, back, up, down, up2, down2
-    )
+    next_rows, return_rows, grad_down, grad_up = settle(wiring, place, fwd, back, up, down)
     return (
         next_rows.reshape(1, 1, rows, width),
         return_rows.reshape(1, 1, rows, width),

time: 224 us -> 220 us (0.982)
  Pallas kernels: 222 us -> 217 us
    pallas_call x1, Pallas kernels: 6.98 us -> 3.44 us  [settle(): pl.pallas_call(settle_kernel, name='settle', in_specs=[hbm] + [vmem] * 5,...]
where the time goes in v4:
time: 220 us; the launch traced here: 218 us
  Pallas kernels  217 us (99%)
    pallas_call x1, Pallas kernels, run_section(): pl.pallas_call(functools.partial(section_kernel, sections, peers), name='...  214 us

profile of v4, /device:TPU:64, one launch (start us, length us, event | category | flops | bytes accessed | tf_op | source)
XLA Modules:
  0.0 218.1 jit_solution(10134166606994827824)
XLA Ops:
  0.6 0.0 copy-start
  0.6 214.0 %section_layer.1 = (bf16[16,8,5120]{2,1,0:T(8,128)(2,1)S(1)}, bf16[16,2,8,5120]{3,2,1,0:T(8,128)(2,1)S(1)}, f32[16,8,5120]{2,1,0:T(8,128)S(1)}, f32[5120,128]{1,0:T(8,128)S(1)}, s32[8,128]{1,0:T(8,128)S(1)}) custom-call(s32[16]{0:T(128)} %masks.1, f32[1,5120]{1,0:T(1,128)} %g_ref.1, s32[16,16,16]{2,1,0:T(8,128)} %wiring.3, bf16[16,8,5120]{2,1,0:T(8,128)(2,1)} %bitcast.8, ...), custom_call_target="tpu_custom_call" | custom-call | tf_op jit(solution)/shard_map/section_layer/pallas_call | solution.py:388
  214.7 0.0 copy-done
  214.7 3.4 %settle.1 = (bf16[16,8,5120]{2,1,0:T(8,128)(2,1)}, bf16[16,8,5120]{2,1,0:T(8,128)(2,1)}, f32[5120,128]{1,0:T(8,128)}, f32[16,8,5120]{2,1,0:T(8,128)}) custom-call(s32[16,16,16]{2,1,0:T(8,128)S(1)} %copy-done, s32[8,128]{1,0:T(8,128)S(1)} %get-tuple-element.13.place, bf16[16,8,5120]{2,1,0:T(8,128)(2,1)S(1)} %get-tuple-element.14.fwd, ...), custom_call_target="tpu_custom_call" | custom-call | tf_op jit(solution)/shard_map/settle/pallas_call | solution.py:463
Async XLA Ops:
  0.6 214.0 %copy-start = (s32[16,16,16]{2,1,0:T(8,128)S(1)}, s32[16,16,16]{2,1,0:T(8,128)}, u32[]{:S(2)}) copy-start(s32[16,16,16]{2,1,0:T(8,128)} %wiring.3) | copy-start | bytes 49156

commit v5 on v4

--- a/solution.py
+++ b/solution.py
@@ -98,7 +98,7 @@
     fwd_out, back_out, gup_out, gdown_out, place_out,
     x_own, dy_own, down_ref, up_ref, x_pack, x_got, dy_got, x_send, dy_send, x_pair, dy_pair,
     x_flat, normed, dns, dxs, fwd, back, gup, gdown, graph_ref, left_ref,
-    counts, tables, load_sem, x1, dy1, x2, dy2, sems_f, sems_b,
+    counts, tables, near, load_sem, x1, dy1, x2, dy2, sems_f, sems_b,
 ):
     section = lax.axis_index("section")
     me = lax.axis_index("peer")
@@ -132,21 +132,20 @@
 
     barrier = pltpu.get_barrier_semaphore()
 
-    @pl.loop(0, peers)
-    def _(t):
-        who = turn(t)
-        for where in (after, ahead):
+    for where in (after, ahead):
+        pl.semaphore_signal(
+            barrier, inc=1, device_id={"section": where, "peer": me}, device_id_type=MESH
+        )
+
+    def greet(semaphore):
+        @pl.loop(1, peers)
+        def _(t):
             pl.semaphore_signal(
-                barrier, inc=1, device_id={"section": where, "peer": who}, device_id_type=MESH
+                semaphore, inc=1, device_id={"section": section, "peer": turn(t)}, device_id_type=MESH
             )
 
-    @pl.loop(1, peers)
-    def _(t):
-        pl.semaphore_signal(
-            barrier, inc=1, device_id={"section": section, "peer": turn(t)}, device_id_type=MESH
-        )
-
-    pl.semaphore_wait(barrier, 3 * peers - 1)
+    greet(barrier)
+    pl.semaphore_wait(barrier, peers + 1)
 
     def remote(src, dst, sems, where, who):
         return pltpu.make_async_remote_copy(
@@ -172,6 +171,8 @@
     def _(t):
         remote(dy_hbm, dy_got, dy1, section, turn(t)).start()
 
+    greet(near)
+
     for copy in loads:
         copy.wait()
 
@@ -241,6 +242,7 @@
         return start + counts[q, me]
 
     lax.fori_loop(0, peers, spread, jnp.int32(0))
+    pl.semaphore_wait(near, peers - 1)
 
     @pl.loop(0, EARLY)
     def _(t):
@@ -405,6 +407,7 @@
             ups, downs, links, links,
             pltpu.SMEM((peers, peers), jnp.int32),
             pltpu.VMEM((2, peers, peers), jnp.int32),
+            pltpu.SemaphoreType.REGULAR,
             dma((8,)),
         ]
         + [dma((2, peers))] * 6,

time: 220 us -> 216 us (0.982)
  no operation moved by 1% of the time
where the time goes in v5:
time: 216 us
  Pallas kernels  216 us (100%)
    pallas_call x1, Pallas kernels, run_section(): pl.pallas_call(functools.partial(section_kernel, sections, peers), name='...  212 us

profile of v5, /device:TPU:64, one launch (start us, length us, event | category | flops | bytes accessed | tf_op | source)
XLA Modules:
  0.0 216.3 jit_solution(9624516411731320620)
XLA Ops:
  0.6 0.0 copy-start
  0.6 212.2 %section_layer.1 = (bf16[16,8,5120]{2,1,0:T(8,128)(2,1)S(1)}, bf16[16,2,8,5120]{3,2,1,0:T(8,128)(2,1)S(1)}, f32[16,8,5120]{2,1,0:T(8,128)S(1)}, f32[5120,128]{1,0:T(8,128)S(1)}, s32[8,128]{1,0:T(8,128)S(1)}) custom-call(s32[16]{0:T(128)} %masks.1, f32[1,5120]{1,0:T(1,128)} %g_ref.1, s32[16,16,16]{2,1,0:T(8,128)} %wiring.3, bf16[16,8,5120]{2,1,0:T(8,128)(2,1)} %bitcast.8, ...), custom_call_target="tpu_custom_call" | custom-call | tf_op jit(solution)/shard_map/section_layer/pallas_call | solution.py:390
  212.9 0.0 copy-done
  212.9 3.4 %settle.1 = (bf16[16,8,5120]{2,1,0:T(8,128)(2,1)}, bf16[16,8,5120]{2,1,0:T(8,128)(2,1)}, f32[5120,128]{1,0:T(8,128)}, f32[16,8,5120]{2,1,0:T(8,128)}) custom-call(s32[16,16,16]{2,1,0:T(8,128)S(1)} %copy-done, s32[8,128]{1,0:T(8,128)S(1)} %get-tuple-element.13.place, bf16[16,8,5120]{2,1,0:T(8,128)(2,1)S(1)} %get-tuple-element.14.fwd, ...), custom_call_target="tpu_custom_call" | custom-call | tf_op jit(solution)/shard_map/settle/pallas_call | solution.py:466
Async XLA Ops:
  0.6 212.2 %copy-start = (s32[16,16,16]{2,1,0:T(8,128)S(1)}, s32[16,16,16]{2,1,0:T(8,128)}, u32[]{:S(2)}) copy-start(s32[16,16,16]{2,1,0:T(8,128)} %wiring.3) | copy-start | bytes 49156

commit v6 on v5

--- a/solution.py
+++ b/solution.py
@@ -9,7 +9,7 @@
 
 CAP = 2
 WIDE = 512
-EARLY = 8
+EARLY = 6
 MESH = pl.DeviceIdType.MESH
 F32, BF16 = jnp.float32, jnp.bfloat16
 
@@ -94,11 +94,11 @@
 
 
 def section_kernel(
-    sections, peers, masks, g_ref, wiring, x_hbm, dy_hbm, down_hbm, up_hbm,
+    sections, peers, masks_in, gains, wiring, x_hbm, dy_hbm, down_hbm, up_hbm,
     fwd_out, back_out, gup_out, gdown_out, place_out,
     x_own, dy_own, down_ref, up_ref, x_pack, x_got, dy_got, x_send, dy_send, x_pair, dy_pair,
     x_flat, normed, dns, dxs, fwd, back, gup, gdown, graph_ref, left_ref,
-    counts, tables, near, load_sem, x1, dy1, x2, dy2, sems_f, sems_b,
+    masks, g_ref, counts, tables, near, load_sem, x1, dy1, x2, dy2, sems_f, sems_b,
 ):
     section = lax.axis_index("section")
     me = lax.axis_index("peer")
@@ -125,11 +125,10 @@
             (wiring.at[section], tables.at[0]),
             (wiring.at[ahead], tables.at[1]),
             (dy_hbm.at[me], dy_got.at[me]),
+            (masks_in, masks),
+            (gains, g_ref),
         ))
     ]
-    for copy in loads:
-        copy.start()
-
     barrier = pltpu.get_barrier_semaphore()
 
     for where in (after, ahead):
@@ -145,6 +144,8 @@
             )
 
     greet(barrier)
+    for copy in loads:
+        copy.start()
     pl.semaphore_wait(barrier, peers + 1)
 
     def remote(src, dst, sems, where, who):
@@ -276,10 +277,6 @@
     def _(t):
         remote(x_pack, x_got, x1, section, turn(t)).start()
 
-    @pl.loop(EARLY, peers)
-    def _(t):
-        remote(back, back_out, sems_b, ahead, turn(t)).start()
-
     @pl.loop(1, peers)
     def _(t):
         arrival(dy_hbm, dy_got, dy1, section, turn(t)).wait_recv()
@@ -317,6 +314,10 @@
     def _(t):
         remote(x_send, x_pair, x2, section, turn(t)).start()
 
+    @pl.loop(EARLY, peers)
+    def _(t):
+        remote(back, back_out, sems_b, ahead, turn(t)).start()
+
     rinv_got = inverse(x_got)
     pre_got = lax.fori_loop(
         0, chunks, lambda c, pre: pre + project(x_got, rinv_got, cols(c))[1], zero
@@ -377,7 +378,6 @@
 
 def run_section(masks, g, wiring, x, dy, down, up, sections, peers):
     vmem = pl.BlockSpec(memory_space=pltpu.VMEM)
-    smem = pl.BlockSpec(memory_space=pltpu.SMEM)
     hbm = pl.BlockSpec(memory_space=pl.ANY)
     dma = pltpu.SemaphoreType.DMA
     blocks, blk, width = x.shape
@@ -390,7 +390,7 @@
     return pl.pallas_call(
         functools.partial(section_kernel, sections, peers),
         name="section_layer",
-        in_specs=[smem, vmem] + [hbm] * 5,
+        in_specs=[hbm] * 7,
         out_specs=[vmem] * 5,
         out_shape=[
             pltpu.VMEM(x.shape, BF16),
@@ -405,10 +405,12 @@
             pltpu.VMEM((rows, width), BF16), pltpu.VMEM((rows, width), F32),
             piece, piece, pltpu.VMEM(slots, BF16),
             ups, downs, links, links,
+            pltpu.SMEM(masks.shape, jnp.int32),
+            pltpu.VMEM(g.shape, F32),
             pltpu.SMEM((peers, peers), jnp.int32),
             pltpu.VMEM((2, peers, peers), jnp.int32),
             pltpu.SemaphoreType.REGULAR,
-            dma((8,)),
+            dma((10,)),
         ]
         + [dma((2, peers))] * 6,
         compiler_params=pltpu.CompilerParams(

time: 216 us -> 215 us (level)
  Pallas kernels: 216 us -> 213 us
    pallas_call x1, Pallas kernels: 212 us -> 209 us  [run_section(): pl.pallas_call(functools.partial(section_kernel, sections, peers), name='...]
where the time goes in v6:
time: 215 us; the launch traced here: 214 us
  Pallas kernels  213 us (99%)
    pallas_call x1, Pallas kernels, run_section(): pl.pallas_call(functools.partial(section_kernel, sections, peers), name='...  209 us

profile of v6, /device:TPU:64, one launch (start us, length us, event | category | flops | bytes accessed | tf_op | source)
XLA Modules:
  0.0 213.5 jit_solution(13156885366949681221)
XLA Ops:
  0.6 0.0 copy-start
  0.6 209.4 %section_layer.1 = (bf16[16,8,5120]{2,1,0:T(8,128)(2,1)S(1)}, bf16[16,2,8,5120]{3,2,1,0:T(8,128)(2,1)S(1)}, f32[16,8,5120]{2,1,0:T(8,128)S(1)}, f32[5120,128]{1,0:T(8,128)S(1)}, s32[8,128]{1,0:T(8,128)S(1)}) custom-call(s32[16]{0:T(128)} %masks_in.1, f32[1,5120]{1,0:T(1,128)} %gains.1, s32[16,16,16]{2,1,0:T(8,128)} %wiring.3, bf16[16,8,5120]{2,1,0:T(8,128)(2,1)} %bitcast.8, ...), custom_call_target="tpu_custom_call" | custom-call | tf_op jit(solution)/shard_map/section_layer/pallas_call | solution.py:390
  210.1 0.0 copy-done
  210.1 3.4 %settle.1 = (bf16[16,8,5120]{2,1,0:T(8,128)(2,1)}, bf16[16,8,5120]{2,1,0:T(8,128)(2,1)}, f32[5120,128]{1,0:T(8,128)}, f32[16,8,5120]{2,1,0:T(8,128)}) custom-call(s32[16,16,16]{2,1,0:T(8,128)S(1)} %copy-done, s32[8,128]{1,0:T(8,128)S(1)} %get-tuple-element.13.place, bf16[16,8,5120]{2,1,0:T(8,128)(2,1)S(1)} %get-tuple-element.14.fwd, ...), custom_call_target="tpu_custom_call" | custom-call | tf_op jit(solution)/shard_map/settle/pallas_call | solution.py:468
Async XLA Ops:
  0.6 209.5 %copy-start = (s32[16,16,16]{2,1,0:T(8,128)S(1)}, s32[16,16,16]{2,1,0:T(8,128)}, u32[]{:S(2)}) copy-start(s32[16,16,16]{2,1,0:T(8,128)} %wiring.3) | copy-start | bytes 49156

commit v7 on v6

--- a/solution.py
+++ b/solution.py
@@ -10,6 +10,7 @@
 CAP = 2
 WIDE = 512
 EARLY = 6
+LATE = 11
 MESH = pl.DeviceIdType.MESH
 F32, BF16 = jnp.float32, jnp.bfloat16
 
@@ -314,7 +315,7 @@
     def _(t):
         remote(x_send, x_pair, x2, section, turn(t)).start()
 
-    @pl.loop(EARLY, peers)
+    @pl.loop(EARLY, LATE)
     def _(t):
         remote(back, back_out, sems_b, ahead, turn(t)).start()
 
@@ -333,8 +334,13 @@
         oc = (wide(x_got, at) + mul(act_got, up_ref[:, at])).astype(BF16)
         fwd[:, :, at] = tall(mul(sorting, oc))
 
-    @pl.loop(0, peers)
-    def _(t):
+    @pl.loop(0, LATE)
+    def _(t):
+        remote(fwd, fwd_out, sems_f, after, turn(t)).start()
+
+    @pl.loop(LATE, peers)
+    def _(t):
+        remote(back, back_out, sems_b, ahead, turn(t)).start()
         remote(fwd, fwd_out, sems_f, after, turn(t)).start()
 
     theirs = order(jnp.bitwise_xor(me, mask))

time: 215 us -> 217 us (level)
  no operation moved by 1% of the time
where the time goes in v7:
time: 217 us; the launch traced here: 216 us
  Pallas kernels  215 us (99%)
    pallas_call x1, Pallas kernels, run_section(): pl.pallas_call(functools.partial(section_kernel, sections, peers), name='...  211 us

profile of v7, /device:TPU:64, one launch (start us, length us, event | category | flops | bytes accessed | tf_op | source)
XLA Modules:
  0.0 215.6 jit_solution(12471309787553069265)
XLA Ops:
  0.6 0.0 copy-start
  0.6 211.5 %section_layer.1 = (bf16[16,8,5120]{2,1,0:T(8,128)(2,1)S(1)}, bf16[16,2,8,5120]{3,2,1,0:T(8,128)(2,1)S(1)}, f32[16,8,5120]{2,1,0:T(8,128)S(1)}, f32[5120,128]{1,0:T(8,128)S(1)}, s32[8,128]{1,0:T(8,128)S(1)}) custom-call(s32[16]{0:T(128)} %masks_in.1, f32[1,5120]{1,0:T(1,128)} %gains.1, s32[16,16,16]{2,1,0:T(8,128)} %wiring.3, bf16[16,8,5120]{2,1,0:T(8,128)(2,1)} %bitcast.8, ...), custom_call_target="tpu_custom_call" | custom-call | tf_op jit(solution)/shard_map/section_layer/pallas_call | solution.py:396
  212.1 0.0 copy-done
  212.1 3.4 %settle.1 = (bf16[16,8,5120]{2,1,0:T(8,128)(2,1)}, bf16[16,8,5120]{2,1,0:T(8,128)(2,1)}, f32[5120,128]{1,0:T(8,128)}, f32[16,8,5120]{2,1,0:T(8,128)}) custom-call(s32[16,16,16]{2,1,0:T(8,128)S(1)} %copy-done, s32[8,128]{1,0:T(8,128)S(1)} %get-tuple-element.13.place, bf16[16,8,5120]{2,1,0:T(8,128)(2,1)S(1)} %get-tuple-element.14.fwd, ...), custom_call_target="tpu_custom_call" | custom-call | tf_op jit(solution)/shard_map/settle/pallas_call | solution.py:474
Async XLA Ops:
  0.6 211.5 %copy-start = (s32[16,16,16]{2,1,0:T(8,128)S(1)}, s32[16,16,16]{2,1,0:T(8,128)}, u32[]{:S(2)}) copy-start(s32[16,16,16]{2,1,0:T(8,128)} %wiring.3) | copy-start | bytes 49156

commit v8 on v6

--- a/solution.py
+++ b/solution.py
@@ -112,6 +112,7 @@
     def turn(t):
         half = (t + 1) // 2
         step = half + (1 - t % 2) * (peers - 2 * half)
+        step = step + lax.rem(section, 2) * (peers - 2 * step)
         return lax.rem(me + step, peers)
 
     loads = [

time: 215 us -> 215 us (level)
  no operation moved by 1% of the time
where the time goes in v8:
time: 215 us; the launch traced here: 214 us
  Pallas kernels  213 us (99%)
    pallas_call x1, Pallas kernels, run_section(): pl.pallas_call(functools.partial(section_kernel, sections, peers), name='...  209 us

profile of v8, /device:TPU:64, one launch (start us, length us, event | category | flops | bytes accessed | tf_op | source)
XLA Modules:
  0.0 213.6 jit_solution(4853545541929233254)
XLA Ops:
  0.6 0.0 copy-start
  0.6 209.5 %section_layer.1 = (bf16[16,8,5120]{2,1,0:T(8,128)(2,1)S(1)}, bf16[16,2,8,5120]{3,2,1,0:T(8,128)(2,1)S(1)}, f32[16,8,5120]{2,1,0:T(8,128)S(1)}, f32[5120,128]{1,0:T(8,128)S(1)}, s32[8,128]{1,0:T(8,128)S(1)}) custom-call(s32[16]{0:T(128)} %masks_in.1, f32[1,5120]{1,0:T(1,128)} %gains.1, s32[16,16,16]{2,1,0:T(8,128)} %wiring.3, bf16[16,8,5120]{2,1,0:T(8,128)(2,1)} %bitcast.8, ...), custom_call_target="tpu_custom_call" | custom-call | tf_op jit(solution)/shard_map/section_layer/pallas_call | solution.py:391
  210.1 0.0 copy-done
  210.1 3.4 %settle.1 = (bf16[16,8,5120]{2,1,0:T(8,128)(2,1)}, bf16[16,8,5120]{2,1,0:T(8,128)(2,1)}, f32[5120,128]{1,0:T(8,128)}, f32[16,8,5120]{2,1,0:T(8,128)}) custom-call(s32[16,16,16]{2,1,0:T(8,128)S(1)} %copy-done, s32[8,128]{1,0:T(8,128)S(1)} %get-tuple-element.13.place, bf16[16,8,5120]{2,1,0:T(8,128)(2,1)S(1)} %get-tuple-element.14.fwd, ...), custom_call_target="tpu_custom_call" | custom-call | tf_op jit(solution)/shard_map/settle/pallas_call | solution.py:469
Async XLA Ops:
  0.6 209.5 %copy-start = (s32[16,16,16]{2,1,0:T(8,128)S(1)}, s32[16,16,16]{2,1,0:T(8,128)}, u32[]{:S(2)}) copy-start(s32[16,16,16]{2,1,0:T(8,128)} %wiring.3) | copy-start | bytes 49156
